TPU v7x, 128 devices: a whole 4x4x4 slice. The times are simulated.
128 devices in a mesh: grp: 4 (over x), tile: 32 (over y, z, core).
Axes of the slice: x: 4, y: 4, z: 4, core: 2. Of those that a mesh axis runs over, the one named last changes fastest.
Arguments:
- profiles: float32 [4, 64, 262144], P(None, None, ('grp', 'tile')), may hold values from -6 to 6
- heat_coupling: float32 [64, 262144], P(None, ('grp', 'tile')), may hold values from 0.1 to 10
- momentum_coupling: float32 [64, 262144], P(None, ('grp', 'tile')), may hold values from 0.1 to 10
- layer_mass: float32 [64, 262144], P(None, ('grp', 'tile')), may hold values from 0.3 to 3
- soil_temps: float32 [8, 1572864], P(None, ('grp', 'tile')), may hold values from -6 to 6
- heat_capacity: float32 [8, 1572864], P(None, ('grp', 'tile')), may hold values from 0.5 to 5
- conductance: float32 [8, 1572864], P(None, ('grp', 'tile')), may hold values from 0.2 to 5
- exchange_coeffs: float32 [3, 1572864], P(None, ('grp', 'tile')), may hold values from 0.2 to 5
- wetness: float32 [1572864], P(('grp', 'tile')), may hold values from -1 to 1
- area_table: float32 [256], replicated, may hold values from 0.05 to 1
- entry_column: int32 [1572864], P(('grp', 'tile')), may hold values from 0 to 2047, as said below
- entry_owner: int32 [1572864], P(('grp', 'tile')), may hold values from 0 to 127, as said below
- entry_cell: int32 [1572864], P(('grp', 'tile')), may hold values from 0 to 12287, as said below
- entry_area: int32 [1572864], P(('grp', 'tile')), may hold values from 0 to 255
- surface_type: int32 [1572864], P(('grp', 'tile')), may hold values from 0 to 3
- layer_counts: int32 [4], replicated, may hold values from 1 to 8
Outputs:
- new_profiles: float32 [4, 64, 262144], P(None, None, ('grp', 'tile'))
- new_soil: float32 [8, 1572864], P(None, ('grp', 'tile'))
Inputs may be any that keep to these rules, and one draw needn't show every extreme that they name: `entry_column`: every column of a device is named by at least one of that device's entries. `entry_owner`: A device's entries name any one owner at most 192 times, and every device names some owner exactly 192 times; every owner is named by exactly 12288 entries over all devices. `entry_cell`: over all devices, the entries that name one owner carry each cell id of that owner exactly once.
All inputs are finite; a program needn't handle non-finite values.
Results may differ from a plain program's by a relative error of at most 0.00005.
Values sent between devices are 32-bit elements; how exact they have to be, the bound alone decides.
A program may use at most 128 MiB of HBM per device.

v0:
```python
import jax
import jax.numpy as jnp
from jax import lax
from jax.experimental import pallas as pl
from jax.experimental.pallas import tpu as pltpu
from jax.sharding import PartitionSpec as P

PEERS = 128
LANES = 128
SLOT_ROWS = 192
MSG_ROWS = 8
BF16 = jnp.bfloat16
F32 = jnp.float32
I32 = jnp.int32
VMEM_LIMIT = 56 * 1024 * 1024


def iota(shape, dim):
    return lax.broadcasted_iota(I32, shape, dim)


def split3(x):
    high = x.astype(BF16).astype(F32)
    rest = x - high
    mid = rest.astype(BF16).astype(F32)
    return high, mid, rest - mid


def lane_gather(table, index):
    return jnp.take_along_axis(table, index, axis=1, mode="promise_in_bounds")


def dot_nt(a, b):
    return lax.dot_general(a, b, (((1,), (1,)), ((), ())), preferred_element_type=F32)


def low_half(shape):
    return iota(shape, 1) < 64


def pack_message(fields, message_ref):
    count = len(fields)
    for f, field_ref in enumerate(fields):
        for g in range(16):
            message_ref[pl.ds(64 * g + f, 8, stride=8), :] = field_ref[8 * g : 8 * g + 8, :]
    for pair in range((count + 1) // 2):
        row = count + pair
        for g in range(8):
            rows = slice(128 + 8 * g, 136 + 8 * g)
            first = fields[2 * pair][rows, :]
            if 2 * pair + 1 < count:
                second = fields[2 * pair + 1][rows, :]
            else:
                second = jnp.zeros_like(first)
            low = low_half(first.shape)
            near = jnp.where(low, first, pltpu.roll(second, 64, 1))
            far = jnp.where(low, pltpu.roll(first, 64, 1), second)
            message_ref[pl.ds(64 * g + row, 8, stride=8), :] = near
            message_ref[pl.ds(64 * (g + 8) + row, 8, stride=8), :] = far


def unpack_message(message_ref, fields):
    count = len(fields)
    for f, field_ref in enumerate(fields):
        for g in range(16):
            field_ref[8 * g : 8 * g + 8, :] = message_ref[pl.ds(64 * g + f, 8, stride=8), :]
    for pair in range((count + 1) // 2):
        row = count + pair
        for g in range(8):
            rows = slice(128 + 8 * g, 136 + 8 * g)
            near = message_ref[pl.ds(64 * g + row, 8, stride=8), :]
            far = message_ref[pl.ds(64 * (g + 8) + row, 8, stride=8), :]
            low = low_half(near.shape)
            fields[2 * pair][rows, :] = jnp.where(low, near, pltpu.roll(far, 64, 1))
            if 2 * pair + 1 < count:
                fields[2 * pair + 1][rows, :] = jnp.where(low, pltpu.roll(near, 64, 1), far)


def assign_slots(owner_ref, pieces_refs, onehot_scr, rank_scr, left_scr, right_scr, acc_scr):
    entry_rows = owner_ref.shape[0]
    upper = (iota((LANES, 2 * LANES), 0) < iota((LANES, 2 * LANES), 1)).astype(F32).astype(BF16)
    owners = iota((PEERS, LANES), 0)

    def rank_body(step, base):
        for q in range(8):
            r = step * 8 + q
            hit = owners == owner_ref[pl.ds(r, 1), :]
            onehot = hit.astype(F32).astype(BF16)
            onehot_scr[:, pl.ds(pl.multiple_of(r * LANES, LANES), LANES)] = onehot
            before = jnp.dot(onehot, upper, preferred_element_type=F32)
            rank_scr[pl.ds(r, 1), :] = jnp.sum(
                jnp.where(hit, before[:, :LANES] + base, 0.0), axis=0, keepdims=True
            )
            base = base + before[:, LANES:]
        return base

    lax.fori_loop(0, entry_rows // 8, rank_body, jnp.zeros((PEERS, LANES), F32))
    acc_scr[...] = jnp.zeros_like(acc_scr)
    ranks = iota((2 * LANES, LANES), 0).astype(F32)

    def scatter_body(step, carry):
        for q in range(8):
            r = step * 8 + q
            onehot = onehot_scr[:, pl.ds(pl.multiple_of(r * LANES, LANES), LANES)]
            for p, piece_ref in enumerate(pieces_refs):
                piece = jnp.broadcast_to(piece_ref[pl.ds(r, 1), :], (PEERS, LANES)).astype(BF16)
                left_scr[p * PEERS : (p + 1) * PEERS, q * LANES : (q + 1) * LANES] = onehot * piece
            right_scr[:, q * LANES : (q + 1) * LANES] = (
                (ranks == rank_scr[pl.ds(r, 1), :]).astype(F32).astype(BF16)
            )
        acc_scr[...] += dot_nt(left_scr[...], right_scr[...])
        return carry

    lax.fori_loop(0, entry_rows // 8, scatter_body, 0)


def slots_of(acc, piece):
    base = piece * PEERS
    for g in range(16):
        yield acc[base + 8 * g : base + 8 * g + 8, 0:LANES]
    for g in range(8):
        near = acc[base + 8 * g : base + 8 * g + 8, LANES : 2 * LANES]
        far = acc[base + 64 + 8 * g : base + 64 + 8 * g + 8, LANES : 2 * LANES]
        yield jnp.where(low_half(near.shape), near, pltpu.roll(far, 64, 1))


def down_sweep(profiles_ref, heat_ref, momentum_ref, mass_ref, factor_ref, reduced_ref, bottom_scr):
    couplings = (heat_ref, momentum_ref)
    zero = jnp.zeros((8, LANES), F32)

    def rows_of(g, i, half):
        return pl.ds(g * 128 + half * 64 + i, 8, stride=8)

    def body(g, carry):
        link, factor, reduced, inverse = carry
        link, factor, reduced, inverse = list(link), list(factor), list(reduced), list(inverse)
        following = jnp.minimum(g + 1, 7)
        keep = (g < 7).astype(F32)
        for i in range(8):
            for half in range(2):
                mass = mass_ref[rows_of(g, i, half), :]
                out_rows = pl.ds(pl.multiple_of(g * 128 + i * 16 + half * 8, 8), 8)
                for pair in range(2):
                    k = 2 * pair + half
                    if i < 7:
                        below = couplings[pair][rows_of(g, i + 1, half), :]
                    else:
                        below = couplings[pair][rows_of(following, 0, half), :] * keep
                    here = link[k]
                    divisor = mass + here + below + here * factor[k]
                    inverse[k] = 1.0 / divisor
                    factor[k] = -below * inverse[k]
                    factor_ref[pair, out_rows, :] = factor[k]
                    for member in range(2):
                        field = 2 * pair + member
                        m = 2 * field + half
                        value = profiles_ref[field, rows_of(g, i, half), :]
                        reduced[m] = (mass * value + here * reduced[m]) * inverse[k]
                        reduced_ref[field, out_rows, :] = reduced[m]
                    link[k] = below
        return tuple(link), tuple(factor), tuple(reduced), tuple(inverse)

    first = tuple(couplings[k // 2][rows_of(0, 0, k % 2), :] for k in range(4))
    _, _, reduced, inverse = lax.fori_loop(
        0, 8, body, (first, (zero,) * 4, (zero,) * 8, (zero,) * 4)
    )
    for half in range(2):
        rows = slice(8 * half, 8 * half + 8)
        for field in range(4):
            bottom_scr[field, rows, :] = reduced[2 * field + half]
        bottom_scr[4, rows, :] = inverse[half]
        bottom_scr[5, rows, :] = inverse[2 + half]


def source_kernel(
    owner_ref, cell_ref, column_ref, area_ref, table_ref, profiles_ref, heat_ref, momentum_ref, mass_ref,
    message_ref, column_slot_ref, weight_slot_ref, wind_slot_ref, factor_ref, reduced_ref, bottom_ref,
    piece_scr, onehot_scr, rank_scr, left_scr, right_scr, acc_scr, field_scr,
):
    down_sweep(profiles_ref, heat_ref, momentum_ref, mass_ref, factor_ref, reduced_ref, bottom_ref)
    cell = cell_ref[...]
    column = column_ref[...]
    piece_scr[0] = ((cell >> 8) + 1).astype(F32)
    piece_scr[1] = (cell & 255).astype(F32)
    piece_scr[2] = (column >> 7).astype(F32)
    piece_scr[3] = (column & 127).astype(F32)
    piece_scr[4] = area_ref[...].astype(F32)
    assign_slots(
        owner_ref, [piece_scr.at[p] for p in range(5)],
        onehot_scr, rank_scr, left_scr, right_scr, acc_scr,
    )
    for g, (cell_high, cell_low, row, lane, area) in enumerate(
        zip(*[slots_of(acc_scr, p) for p in range(5)])
    ):
        rows = slice(8 * g, 8 * g + 8)
        field_scr[0, rows, :] = cell_high * 256.0 + cell_low
        row, lane, area = row.astype(I32), lane.astype(I32), area.astype(I32)
        column_slot_ref[rows, :] = row * LANES + lane
        near = lane_gather(jnp.broadcast_to(table_ref[0:1, :], (8, LANES)), area & 127)
        far = lane_gather(jnp.broadcast_to(table_ref[1:2, :], (8, LANES)), area & 127)
        weight = jnp.where(area < LANES, near, far)
        weight_slot_ref[rows, :] = jnp.where(cell_high > 0.0, weight, 0.0)

    def expand(step, carry):
        index = [column_slot_ref[pl.ds(pl.multiple_of(step * 32 + 8 * j, 8), 8), :] for j in range(4)]
        high = [x >> 7 for x in index]
        low = [x & 127 for x in index]
        totals = [[jnp.zeros((8, LANES), F32) for _ in range(4)] for _ in range(4)]
        for h in range(16):
            tables = [
                jnp.broadcast_to(bottom_ref[f, h : h + 1, :], (8, LANES)) for f in (0, 1, 4, 5)
            ]
            for j in range(4):
                hit = high[j] == h
                for f in range(4):
                    totals[j][f] = jnp.where(hit, lane_gather(tables[f], low[j]), totals[j][f])
        for j in range(4):
            rows = pl.ds(pl.multiple_of(step * 32 + 8 * j, 8), 8)
            for f in range(3):
                field_scr[f + 1, rows, :] = totals[j][f]
            wind_slot_ref[rows, :] = totals[j][3]
        return carry

    lax.fori_loop(0, 6, expand, 0)
    pack_message([field_scr.at[f] for f in range(4)], message_ref)


def soil_block(a, b, soil_ref, capacity_ref, conductance_ref, exchange_ref, wetness_ref, type_ref, counts_ref,
               cells_scr, soil_out_ref, table_scr):
    tiles = pl.ds(16 * a + b, 8, stride=2)
    here = (pl.ds(pl.multiple_of(8 * a, 8), 8), slice(LANES * b, LANES * b + LANES))
    bottom_t = cells_scr[0][here]
    bottom_q = cells_scr[1][here]
    heat_scale = cells_scr[2][here]
    kind = type_ref[tiles, :]
    total = jnp.zeros((8, LANES), I32)
    for t in range(4):
        total = jnp.where(kind == t, counts_ref[t], total)
    heat, moist, drag = (exchange_ref[i, tiles, :] for i in range(3))
    gain_t = heat / (1.0 + heat * heat_scale)
    gain_q = moist / (1.0 + moist * heat_scale)
    link_prev = factor = reduced = None
    factors, reduceds = [], []
    for layer in range(8):
        rows = pl.ds((16 * a + b) * 8 + layer, 8, stride=16)
        conductance = conductance_ref[rows, :]
        capacity = capacity_ref[rows, :]
        link = jnp.where(total > layer + 1, conductance, 0.0)
        deep = jnp.where(total == layer + 1, conductance, 0.0)
        diagonal = capacity + link + deep
        rhs = capacity * soil_ref[rows, :]
        if layer == 0:
            divisor = diagonal + gain_t
            rhs = rhs + gain_t * bottom_t
        else:
            divisor = diagonal + link_prev + link_prev * factor
            rhs = rhs + link_prev * reduced
        inverse = 1.0 / divisor
        factor = -link * inverse
        reduced = rhs * inverse
        factors.append(factor)
        reduceds.append(reduced)
        link_prev = link
    value = None
    for layer in range(7, -1, -1):
        rows = pl.ds((16 * a + b) * 8 + layer, 8, stride=16)
        value = reduceds[layer] if layer == 7 else reduceds[layer] - factors[layer] * value
        kept = value if layer == 0 else jnp.where(total > layer, value, soil_ref[rows, :])
        soil_out_ref[rows, :] = kept
    table_scr[0, tiles, :] = gain_t * (value - bottom_t)
    table_scr[1, tiles, :] = gain_q * (wetness_ref[tiles, :] + 0.5 * value - bottom_q)
    table_scr[2, tiles, :] = drag


def owner_kernel(
    counts_ref, message_ref, soil_ref, capacity_ref, conductance_ref, exchange_ref, wetness_ref, type_ref,
    reply_ref, soil_out_ref,
    field_scr, piece_scr, left_scr, right_scr, acc_scr, cells_scr, table_scr, index_scr,
):
    unpack_message(message_ref, [field_scr.at[f] for f in range(4)])
    index_scr[...] = field_scr[0].astype(I32) - 256
    for f in range(3):
        for p, piece in enumerate(split3(field_scr[f + 1])):
            piece_scr[3 * f + p] = piece
    acc_scr[...] = jnp.zeros_like(acc_scr)
    highs = iota((48, LANES), 0)
    lows = iota((256, LANES), 0)

    def scatter_body(step, carry):
        for q in range(8):
            r = step * 8 + q
            cell = index_scr[pl.ds(r, 1), :]
            lanes = slice(q * LANES, (q + 1) * LANES)
            right_scr[:, lanes] = (lows == (cell & 255)).astype(F32).astype(BF16)
            onehot = (highs == (cell >> 8)).astype(F32).astype(BF16)
            for p in range(9):
                piece = jnp.broadcast_to(piece_scr[p, pl.ds(r, 1), :], (48, LANES)).astype(BF16)
                left_scr[48 * p : 48 * p + 48, lanes] = onehot * piece
        acc_scr[...] += dot_nt(left_scr[...], right_scr[...])
        return carry

    lax.fori_loop(0, SLOT_ROWS // 8, scatter_body, 0)
    for f in range(3):
        base = 144 * f
        cells_scr[f] = (
            acc_scr[base : base + 48] + acc_scr[base + 48 : base + 96] + acc_scr[base + 96 : base + 144]
        )

    def soil_body(a, carry):
        for b in range(2):
            soil_block(
                a, b, soil_ref, capacity_ref, conductance_ref, exchange_ref, wetness_ref, type_ref,
                counts_ref, [cells_scr.at[f] for f in range(3)], soil_out_ref, table_scr,
            )
        return carry

    lax.fori_loop(0, 6, soil_body, 0)

    def gather_step(step, carry):
        index = [index_scr[pl.ds(pl.multiple_of(step * 48 + 8 * j, 8), 8), :] for j in range(6)]
        high = [x >> 7 for x in index]
        low = [x & 127 for x in index]

        def row_body(four, totals):
            totals = [list(x) for x in totals]
            for u in range(4):
                h = four * 4 + u
                tables = [
                    jnp.broadcast_to(table_scr[f, pl.ds(h, 1), :], (8, LANES)) for f in range(3)
                ]
                for j in range(6):
                    hit = high[j] == h
                    for f in range(3):
                        totals[j][f] = jnp.where(hit, lane_gather(tables[f], low[j]), totals[j][f])
            return tuple(tuple(x) for x in totals)

        zero = jnp.zeros((8, LANES), F32)
        totals = lax.fori_loop(0, 24, row_body, ((zero,) * 3,) * 6)
        for j in range(6):
            rows = pl.ds(pl.multiple_of(step * 48 + 8 * j, 8), 8)
            for f in range(3):
                field_scr[f, rows, :] = totals[j][f]
        return carry

    lax.fori_loop(0, 4, gather_step, 0)
    pack_message([field_scr.at[f] for f in range(3)], reply_ref)


def column_kernel(
    reply_ref, column_slot_ref, weight_slot_ref, wind_slot_ref, factor_ref, reduced_ref, bottom_ref,
    out_ref,
    field_scr, piece_scr, left_scr, right_scr, acc_scr,
):
    unpack_message(reply_ref, [field_scr.at[f] for f in range(3)])
    weight = weight_slot_ref[...]
    drag = field_scr[2]
    values = (
        weight * field_scr[0],
        weight * field_scr[1],
        weight * (drag / (1.0 + drag * wind_slot_ref[...])),
        weight,
    )
    for f in range(4):
        for p, piece in enumerate(split3(values[f])):
            piece_scr[3 * f + p] = piece
    acc_scr[...] = jnp.zeros_like(acc_scr)
    highs = iota((16, LANES), 0)
    lows = iota((LANES, LANES), 0)

    def scatter_body(step, carry):
        for q in range(8):
            r = step * 8 + q
            column = column_slot_ref[pl.ds(r, 1), :]
            lanes = slice(q * LANES, (q + 1) * LANES)
            right_scr[:, lanes] = (lows == (column & 127)).astype(F32).astype(BF16)
            onehot = (highs == (column >> 7)).astype(F32).astype(BF16)
            for p in range(12):
                piece = jnp.broadcast_to(piece_scr[p, pl.ds(r, 1), :], (16, LANES)).astype(BF16)
                left_scr[16 * p : 16 * p + 16, lanes] = onehot * piece
        acc_scr[...] += dot_nt(left_scr[...], right_scr[...])
        return carry

    lax.fori_loop(0, SLOT_ROWS // 8, scatter_body, 0)
    sums = []
    for f in range(4):
        base = 48 * f
        sums.append(acc_scr[base : base + 16] + acc_scr[base + 16 : base + 32] + acc_scr[base + 32 : base + 48])
    flux = (
        sums[0] / sums[3],
        sums[1] / sums[3],
        -bottom_ref[2] * (sums[2] / sums[3]),
        -bottom_ref[3] * (sums[2] / sums[3]),
    )
    values = []
    for field in range(4):
        lowest = bottom_ref[field] + bottom_ref[4 + field // 2] * flux[field]
        for half in range(2):
            value = lowest[8 * half : 8 * half + 8]
            out_ref[field, pl.ds(7 * 128 + half * 64 + 7, 8, stride=8), :] = value
            values.append(value)

    def retreat(values, g, i):
        values = list(values)
        for half in range(2):
            rows = pl.ds(pl.multiple_of(g * 128 + i * 16 + half * 8, 8), 8)
            for field in range(4):
                k = 2 * field + half
                values[k] = reduced_ref[field, rows, :] - factor_ref[field // 2, rows, :] * values[k]
                out_ref[field, pl.ds(g * 128 + half * 64 + i, 8, stride=8), :] = values[k]
        return tuple(values)

    values = tuple(values)
    for i in range(6, -1, -1):
        values = retreat(values, 7, i)

    def body(step, values):
        for i in range(7, -1, -1):
            values = retreat(values, 6 - step, i)
        return values

    lax.fori_loop(0, 7, body, values)


def call(kernel, out_shapes, scratch, in_specs, **params):
    return pl.pallas_call(
        kernel,
        out_shape=out_shapes,
        in_specs=in_specs,
        out_specs=[pl.BlockSpec(memory_space=pltpu.VMEM)] * len(out_shapes),
        scratch_shapes=scratch,
        compiler_params=pltpu.CompilerParams(vmem_limit_bytes=VMEM_LIMIT, **params),
    )


def tiles_of(x):
    *lead, rows, lanes = x.shape
    x = x.reshape(*lead, rows // 8, 8, lanes // LANES, LANES)
    return jnp.swapaxes(x, -3, -2).reshape(*lead, rows * lanes // LANES, LANES)


def untile(x, rows, lanes):
    *lead, _, _ = x.shape
    x = x.reshape(*lead, rows // 8, lanes // LANES, 8, LANES)
    return jnp.swapaxes(x, -3, -2).reshape(*lead, rows, lanes)


def exchange(message):
    blocks = message.reshape(PEERS, MSG_ROWS, LANES)
    return lax.all_to_all(blocks, ("grp", "tile"), split_axis=0, concat_axis=0, tiled=True).reshape(
        message.shape
    )


def local(
    profiles, heat_coupling, momentum_coupling, layer_mass, soil_temps, heat_capacity, conductance,
    exchange_coeffs, wetness, area_table, entry_column, entry_owner, entry_cell, entry_area,
    surface_type, layer_counts,
):
    shape = jax.ShapeDtypeStruct
    vmem = pl.BlockSpec(memory_space=pltpu.VMEM)
    smem = pl.BlockSpec(memory_space=pltpu.SMEM)
    flat = lambda x: x.reshape(-1, LANES)
    message, column_slot, weight_slot, wind_slot, factor, reduced, bottom = call(
        source_kernel,
        [
            shape((PEERS * MSG_ROWS, LANES), F32),
            shape((SLOT_ROWS, LANES), I32),
            shape((SLOT_ROWS, LANES), F32),
            shape((SLOT_ROWS, LANES), F32),
            shape((2, 1024, LANES), F32),
            shape((4, 1024, LANES), F32),
            shape((6, 16, LANES), F32),
        ],
        [
            pltpu.VMEM((5, 96, LANES), F32),
            pltpu.VMEM((PEERS, 96 * LANES), BF16),
            pltpu.VMEM((96, LANES), F32),
            pltpu.VMEM((5 * PEERS, 1024), BF16),
            pltpu.VMEM((256, 1024), BF16),
            pltpu.VMEM((5 * PEERS, 256), F32),
            pltpu.VMEM((4, SLOT_ROWS, LANES), F32),
        ],
        [vmem] * 9,
    )(
        flat(entry_owner), flat(entry_cell), flat(entry_column), flat(entry_area), flat(area_table),
        tiles_of(profiles), tiles_of(heat_coupling), tiles_of(momentum_coupling), tiles_of(layer_mass),
    )
    received = exchange(message)
    reply, new_soil = call(
        owner_kernel,
        [shape((PEERS * MSG_ROWS, LANES), F32), shape((768, LANES), F32)],
        [
            pltpu.VMEM((4, SLOT_ROWS, LANES), F32),
            pltpu.VMEM((9, SLOT_ROWS, LANES), F32),
            pltpu.VMEM((432, 1024), BF16),
            pltpu.VMEM((256, 1024), BF16),
            pltpu.VMEM((432, 256), F32),
            pltpu.VMEM((3, 48, 256), F32),
            pltpu.VMEM((3, 96, LANES), F32),
            pltpu.VMEM((SLOT_ROWS, LANES), I32),
        ],
        [smem] + [vmem] * 7,
    )(
        layer_counts, received, tiles_of(soil_temps), tiles_of(heat_capacity), tiles_of(conductance),
        exchange_coeffs.reshape(3, 96, LANES), flat(wetness), flat(surface_type),
    )
    returned = exchange(reply)
    (new_profiles,) = call(
        column_kernel,
        [shape((4, 1024, LANES), F32)],
        [
            pltpu.VMEM((3, SLOT_ROWS, LANES), F32),
            pltpu.VMEM((12, SLOT_ROWS, LANES), F32),
            pltpu.VMEM((192, 1024), BF16),
            pltpu.VMEM((LANES, 1024), BF16),
            pltpu.VMEM((192, LANES), F32),
        ],
        [vmem] * 7,
    )(returned, column_slot, weight_slot, wind_slot, factor, reduced, bottom)
    return untile(new_profiles, 64, 2048), untile(new_soil, 8, 12288)


def solution(mesh):
    split = ("grp", "tile")
    return jax.shard_map(
        local,
        mesh=mesh,
        in_specs=(
            P(None, None, split), P(None, split), P(None, split), P(None, split), P(None, split),
            P(None, split), P(None, split), P(None, split), P(split), P(), P(split), P(split),
            P(split), P(split), P(split), P(),
        ),
        out_specs=(P(None, None, split), P(None, split)),
        check_vma=False,
    )
```

profile of v0, /device:TPU:1, one launch (start us, length us, event | category | flops | bytes accessed | tf_op | source)
XLA Modules:
  0.0 117.6 jit_solution(9683570466202542301)
XLA Ops:
  0.6 0.0 copy-start.1
  0.6 20.9 %shard_map.167 = (f32[1024,128]{1,0:T(8,128)}, s32[192,128]{1,0:T(8,128)}, f32[192,128]{1,0:T(8,128)}, f32[192,128]{1,0:T(8,128)}, f32[2,1024,128]{2,1,0:T(8,128...) custom-call(s32[96,128]{1,0:T(8,128)} %bitcast.74, s32[96,128]{1,0:T(8,128)} %bitcast.75, s32[96,128]{1,0:T(8,128)} %bitcast.76, ...), custom_call_target="tpu_custom_call" | custom-call | tf_op jit(solution)/shard_map/pallas_call | solution.py:463
  21.6 11.5 %all-to-all-start = ((f32[128,8,128]{2,1,0:T(8,128)}), f32[128,8,128]{2,1,0:T(8,128)S(1)}, u32[]{:S(2)}, u32[]{:S(2)}) async-start(f32[128,8,128]{2,1,0:T(8,128)} %bitcast.65), calls=%async_computation | async-start | bytes 1048576 | tf_op jit(solution)/shard_map/all_to_all | solution.py:449
  33.1 0.0 copy-done.1
  33.1 0.7 copy.20
  33.7 13.0 %all-to-all-done = f32[128,8,128]{2,1,0:T(8,128)S(1)} async-done(((f32[128,8,128]{2,1,0:T(8,128)}), f32[128,8,128]{2,1,0:T(8,128)S(1)}, u32[]{:S(2)}, u32[]{:S(2)}) %all-to-all-start) | async-done | bytes 524320 | tf_op jit(solution)/shard_map/all_to_all | solution.py:449
  46.7 0.0 copy-start
  46.7 0.8 copy-done
  47.5 38.1 %shard_map.168 = (f32[1024,128]{1,0:T(8,128)}, f32[768,128]{1,0:T(8,128)}) custom-call(s32[4]{0:T(128)} %counts_ref.1, f32[1024,128]{1,0:T(8,128)} %bitcast.61, f32[768,128]{1,0:T(8,128)} %bitcast.70, f32[768,128]{1,0:T(8,128)} %bitcast.71, f32[768,128]{1,0:T(8,128)} %bitcast.72, f32[3,96,128]{2,1,0:T(8,128)} %bitcast.64, f32[96,128]{1,0:T(8,128)} %bitcast.78, ...), custom_call_target="tpu_custom_call" | custom-call | tf_op jit(solution)/shard_map/pallas_call | solution.py:489
  85.7 19.3 %all_to_all.10 = f32[128,8,128]{2,1,0:T(8,128)} all-to-all(f32[128,8,128]{2,1,0:T(8,128)} %bitcast.66), channel_id=1, replica_groups=mesh['grp'=4,'tile'=32] {'grp','tile'}, dimensions={0} | all-to-all | bytes 1048576 | tf_op jit(solution)/shard_map/all_to_all | solution.py:449
  105.0 12.7 %shard_map.169 = f32[4,1024,128]{2,1,0:T(8,128)} custom-call(f32[1024,128]{1,0:T(8,128)} %bitcast.62, s32[192,128]{1,0:T(8,128)} %get-tuple-element.13.column_slot_ref, f32[192,128]{1,0:T(8,128)} %get-tuple-element.14.weight_slot_ref, f32[192,128]{1,0:T(8,128)} %get-tuple-element.15.wind_slot_ref, f32[2,1024,128]{2,1,0:T(8,128)} %get-tuple-element.16.factor_ref, ...), custom_call_target="tpu_custom_call" | custom-call | tf_op jit(solution)/shard_map/pallas_call | solution.py:508
Async XLA Ops:
  0.6 32.4 %copy-start.1 = (f32[3,12288]{1,0:T(4,128)S(1)}, f32[3,12288]{1,0:T(4,128)}, u32[]{:S(2)}) copy-start(f32[3,12288]{1,0:T(4,128)} %param.23) | copy-start | bytes 442372
  21.6 25.2 %all-to-all-start = ((f32[128,8,128]{2,1,0:T(8,128)}), f32[128,8,128]{2,1,0:T(8,128)S(1)}, u32[]{:S(2)}, u32[]{:S(2)}) async-start(f32[128,8,128]{2,1,0:T(8,128)} %bitcast.65), calls=%async_computation | async-start | bytes 1048576 | tf_op jit(solution)/shard_map/all_to_all | solution.py:449
  46.7 0.8 copy-start
where the time goes:
time: 118 us
  Pallas kernels  71.7 us (61%)
  blocking collectives  19.3 us (16%)
  waiting for transfers between devices  13 us (11%)
  starting transfers between devices  11.5 us (10%)
  local copies, waits for them, and re-layouts  1.46 us (1%)
    pallas_call x1, Pallas kernels, local(): call(owner_kernel, [shape((PEERS * MSG_ROWS, LANES), F32), shape((768, LA...  38.1 us
    pallas_call x1, Pallas kernels, local(): call(source_kernel, [shape((PEERS * MSG_ROWS, LANES), F32), shape((SLOT_R...  20.9 us
    all_to_all x1, blocking collectives, exchange(): lax.all_to_all(blocks, ('grp', 'tile'), split_axis=0, concat_axis=0, tile...  19.3 us
    all_to_all x1, waiting for transfers between devices, exchange(): lax.all_to_all(blocks, ('grp', 'tile'), split_axis=0, concat_axis=0, tile...  13 us
    pallas_call x1, Pallas kernels, local(): call(column_kernel, [shape((4, 1024, LANES), F32)], [pltpu.VMEM((3, SLOT_...  12.7 us
    all_to_all x1, starting transfers between devices, exchange(): lax.all_to_all(blocks, ('grp', 'tile'), split_axis=0, concat_axis=0, tile...  11.5 us
  transfers between devices with their start and end apart: 1, of which 1 were waited for; matrix products, arithmetic and copies ran while one was open for 1% of the time, Pallas kernels for 0%

commit v1 on v0

--- a/solution.py
+++ b/solution.py
@@ -9,6 +9,8 @@
 LANES = 128
 SLOT_ROWS = 192
 MSG_ROWS = 8
+SEND_ROWS = 6
+REPLY_ROWS = 5
 BF16 = jnp.bfloat16
 F32 = jnp.float32
 I32 = jnp.int32
@@ -172,12 +174,7 @@
         bottom_scr[5, rows, :] = inverse[2 + half]
 
 
-def source_kernel(
-    owner_ref, cell_ref, column_ref, area_ref, table_ref, profiles_ref, heat_ref, momentum_ref, mass_ref,
-    message_ref, column_slot_ref, weight_slot_ref, wind_slot_ref, factor_ref, reduced_ref, bottom_ref,
-    piece_scr, onehot_scr, rank_scr, left_scr, right_scr, acc_scr, field_scr,
-):
-    down_sweep(profiles_ref, heat_ref, momentum_ref, mass_ref, factor_ref, reduced_ref, bottom_ref)
+def prepare_pieces(cell_ref, column_ref, area_ref, piece_scr):
     cell = cell_ref[...]
     column = column_ref[...]
     piece_scr[0] = ((cell >> 8) + 1).astype(F32)
@@ -185,15 +182,14 @@
     piece_scr[2] = (column >> 7).astype(F32)
     piece_scr[3] = (column & 127).astype(F32)
     piece_scr[4] = area_ref[...].astype(F32)
-    assign_slots(
-        owner_ref, [piece_scr.at[p] for p in range(5)],
-        onehot_scr, rank_scr, left_scr, right_scr, acc_scr,
-    )
+
+
+def read_slots(acc_scr, table_ref, id_ref, column_slot_ref, weight_slot_ref):
     for g, (cell_high, cell_low, row, lane, area) in enumerate(
         zip(*[slots_of(acc_scr, p) for p in range(5)])
     ):
         rows = slice(8 * g, 8 * g + 8)
-        field_scr[0, rows, :] = cell_high * 256.0 + cell_low
+        id_ref[rows, :] = cell_high * 256.0 + cell_low
         row, lane, area = row.astype(I32), lane.astype(I32), area.astype(I32)
         column_slot_ref[rows, :] = row * LANES + lane
         near = lane_gather(jnp.broadcast_to(table_ref[0:1, :], (8, LANES)), area & 127)
@@ -201,6 +197,8 @@
         weight = jnp.where(area < LANES, near, far)
         weight_slot_ref[rows, :] = jnp.where(cell_high > 0.0, weight, 0.0)
 
+
+def expand_columns(bottom_ref, column_slot_ref, field_scr, wind_slot_ref):
     def expand(step, carry):
         index = [column_slot_ref[pl.ds(pl.multiple_of(step * 32 + 8 * j, 8), 8), :] for j in range(4)]
         high = [x >> 7 for x in index]
@@ -222,7 +220,6 @@
         return carry
 
     lax.fori_loop(0, 6, expand, 0)
-    pack_message([field_scr.at[f] for f in range(4)], message_ref)
 
 
 def soil_block(a, b, soil_ref, capacity_ref, conductance_ref, exchange_ref, wetness_ref, type_ref, counts_ref,
@@ -272,12 +269,7 @@
     table_scr[2, tiles, :] = drag
 
 
-def owner_kernel(
-    counts_ref, message_ref, soil_ref, capacity_ref, conductance_ref, exchange_ref, wetness_ref, type_ref,
-    reply_ref, soil_out_ref,
-    field_scr, piece_scr, left_scr, right_scr, acc_scr, cells_scr, table_scr, index_scr,
-):
-    unpack_message(message_ref, [field_scr.at[f] for f in range(4)])
+def cells_of_slots(index_scr, field_scr, piece_scr, left_scr, right_scr, acc_scr, cells_scr):
     index_scr[...] = field_scr[0].astype(I32) - 256
     for f in range(3):
         for p, piece in enumerate(split3(field_scr[f + 1])):
@@ -306,16 +298,17 @@
             acc_scr[base : base + 48] + acc_scr[base + 48 : base + 96] + acc_scr[base + 96 : base + 144]
         )
 
+
+def solve_soil(*refs):
     def soil_body(a, carry):
         for b in range(2):
-            soil_block(
-                a, b, soil_ref, capacity_ref, conductance_ref, exchange_ref, wetness_ref, type_ref,
-                counts_ref, [cells_scr.at[f] for f in range(3)], soil_out_ref, table_scr,
-            )
+            soil_block(a, b, *refs)
         return carry
 
     lax.fori_loop(0, 6, soil_body, 0)
 
+
+def slots_of_cells(index_scr, table_scr, field_scr):
     def gather_step(step, carry):
         index = [index_scr[pl.ds(pl.multiple_of(step * 48 + 8 * j, 8), 8), :] for j in range(6)]
         high = [x >> 7 for x in index]
@@ -343,15 +336,11 @@
         return carry
 
     lax.fori_loop(0, 4, gather_step, 0)
-    pack_message([field_scr.at[f] for f in range(3)], reply_ref)
-
-
-def column_kernel(
-    reply_ref, column_slot_ref, weight_slot_ref, wind_slot_ref, factor_ref, reduced_ref, bottom_ref,
-    out_ref,
-    field_scr, piece_scr, left_scr, right_scr, acc_scr,
+
+
+def column_sums(
+    column_slot_ref, weight_slot_ref, wind_slot_ref, field_scr, piece_scr, left_scr, right_scr, acc_scr
 ):
-    unpack_message(reply_ref, [field_scr.at[f] for f in range(3)])
     weight = weight_slot_ref[...]
     drag = field_scr[2]
     values = (
@@ -385,6 +374,10 @@
     for f in range(4):
         base = 48 * f
         sums.append(acc_scr[base : base + 16] + acc_scr[base + 16 : base + 32] + acc_scr[base + 32 : base + 48])
+    return sums
+
+
+def up_sweep(sums, factor_ref, reduced_ref, bottom_ref, out_ref):
     flux = (
         sums[0] / sums[3],
         sums[1] / sums[3],
@@ -421,6 +414,95 @@
     lax.fori_loop(0, 7, body, values)
 
 
+def device_of(peer):
+    return (peer // 32, lax.rem(peer, 32))
+
+
+def greet(me):
+    barrier = pltpu.get_barrier_semaphore()
+
+    def signal(d, carry):
+        pl.semaphore_signal(
+            barrier, inc=1, device_id=device_of(lax.rem(me + d, PEERS)),
+            device_id_type=pl.DeviceIdType.MESH,
+        )
+        return carry
+
+    lax.fori_loop(1, PEERS, signal, 0)
+
+
+def send_all(me, send_ref, recv_ref, rows, send_sem, recv_sem):
+    def start(d, carry):
+        peer = lax.rem(me + d, PEERS)
+        pltpu.make_async_remote_copy(
+            src_ref=send_ref.at[pl.ds(pl.multiple_of(peer * MSG_ROWS, MSG_ROWS), rows)],
+            dst_ref=recv_ref.at[pl.ds(pl.multiple_of(me * MSG_ROWS, MSG_ROWS), rows)],
+            send_sem=send_sem, recv_sem=recv_sem, device_id=device_of(peer),
+            device_id_type=pl.DeviceIdType.MESH,
+        ).start()
+        return carry
+
+    lax.fori_loop(1, PEERS, start, 0)
+    own = pl.ds(pl.multiple_of(me * MSG_ROWS, MSG_ROWS), MSG_ROWS)
+    recv_ref[own, :] = send_ref[own, :]
+
+
+def all_of(me, send_ref, recv_ref, rows, send_sem, recv_sem):
+    whole = pl.ds(0, (PEERS - 1) * rows)
+    return pltpu.make_async_remote_copy(
+        src_ref=send_ref.at[whole], dst_ref=recv_ref.at[whole], send_sem=send_sem, recv_sem=recv_sem,
+        device_id=device_of(me), device_id_type=pl.DeviceIdType.MESH,
+    )
+
+
+def step_kernel(
+    owner_ref, cell_ref, column_ref, area_ref, table_ref, profiles_ref, heat_ref, momentum_ref, mass_ref,
+    counts_ref, soil_ref, capacity_ref, conductance_ref, exchange_ref, wetness_ref, type_ref,
+    out_ref, soil_out_ref,
+    column_slot_scr, weight_slot_scr, wind_slot_scr, factor_scr, reduced_scr, bottom_scr,
+    piece_scr, onehot_scr, rank_scr, left_scr, right_scr, slot_acc_scr, field_scr,
+    slot_piece_scr, cell_acc_scr, cells_scr, table_scr, index_scr, column_acc_scr,
+    send_scr, recv_scr, reply_scr, return_scr, sems,
+):
+    me = lax.axis_index("grp") * 32 + lax.axis_index("tile")
+    greet(me)
+    prepare_pieces(cell_ref, column_ref, area_ref, piece_scr)
+    assign_slots(
+        owner_ref, [piece_scr.at[p] for p in range(5)],
+        onehot_scr, rank_scr, left_scr, right_scr, slot_acc_scr,
+    )
+    read_slots(slot_acc_scr, table_ref, field_scr.at[0], column_slot_scr, weight_slot_scr)
+    down_sweep(profiles_ref, heat_ref, momentum_ref, mass_ref, factor_scr, reduced_scr, bottom_scr)
+    expand_columns(bottom_scr, column_slot_scr, field_scr, wind_slot_scr)
+    fields = [field_scr.at[f] for f in range(4)]
+    pack_message(fields, send_scr)
+    pl.semaphore_wait(pltpu.get_barrier_semaphore(), PEERS - 1)
+    send_all(me, send_scr, recv_scr, SEND_ROWS, sems.at[0], sems.at[1])
+    there = all_of(me, send_scr, recv_scr, SEND_ROWS, sems.at[0], sems.at[1])
+    there.wait_recv()
+    unpack_message(recv_scr, fields)
+    cells_of_slots(
+        index_scr, field_scr, slot_piece_scr, left_scr.at[0:432], right_scr, cell_acc_scr, cells_scr
+    )
+    solve_soil(
+        soil_ref, capacity_ref, conductance_ref, exchange_ref, wetness_ref, type_ref, counts_ref,
+        [cells_scr.at[f] for f in range(3)], soil_out_ref, table_scr,
+    )
+    slots_of_cells(index_scr, table_scr, field_scr)
+    pack_message(fields[:3], reply_scr)
+    send_all(me, reply_scr, return_scr, REPLY_ROWS, sems.at[2], sems.at[3])
+    back = all_of(me, reply_scr, return_scr, REPLY_ROWS, sems.at[2], sems.at[3])
+    back.wait_recv()
+    unpack_message(return_scr, fields[:3])
+    sums = column_sums(
+        column_slot_scr, weight_slot_scr, wind_slot_scr, field_scr, slot_piece_scr,
+        left_scr.at[0:192], right_scr.at[0:LANES], column_acc_scr,
+    )
+    up_sweep(sums, factor_scr, reduced_scr, bottom_scr, out_ref)
+    there.wait_send()
+    back.wait_send()
+
+
 def call(kernel, out_shapes, scratch, in_specs, **params):
     return pl.pallas_call(
         kernel,
@@ -442,13 +524,6 @@
     *lead, _, _ = x.shape
     x = x.reshape(*lead, rows // 8, lanes // LANES, 8, LANES)
     return jnp.swapaxes(x, -3, -2).reshape(*lead, rows, lanes)
-
-
-def exchange(message):
-    blocks = message.reshape(PEERS, MSG_ROWS, LANES)
-    return lax.all_to_all(blocks, ("grp", "tile"), split_axis=0, concat_axis=0, tiled=True).reshape(
-        message.shape
-    )
 
 
 def local(
@@ -460,63 +535,42 @@
     vmem = pl.BlockSpec(memory_space=pltpu.VMEM)
     smem = pl.BlockSpec(memory_space=pltpu.SMEM)
     flat = lambda x: x.reshape(-1, LANES)
-    message, column_slot, weight_slot, wind_slot, factor, reduced, bottom = call(
-        source_kernel,
+    slots = (SLOT_ROWS, LANES)
+    messages = pltpu.VMEM((PEERS * MSG_ROWS, LANES), F32)
+    new_profiles, new_soil = call(
+        step_kernel,
+        [shape((4, 1024, LANES), F32), shape((768, LANES), F32)],
         [
-            shape((PEERS * MSG_ROWS, LANES), F32),
-            shape((SLOT_ROWS, LANES), I32),
-            shape((SLOT_ROWS, LANES), F32),
-            shape((SLOT_ROWS, LANES), F32),
-            shape((2, 1024, LANES), F32),
-            shape((4, 1024, LANES), F32),
-            shape((6, 16, LANES), F32),
-        ],
-        [
+            pltpu.VMEM(slots, I32),
+            pltpu.VMEM(slots, F32),
+            pltpu.VMEM(slots, F32),
+            pltpu.VMEM((2, 1024, LANES), F32),
+            pltpu.VMEM((4, 1024, LANES), F32),
+            pltpu.VMEM((6, 16, LANES), F32),
             pltpu.VMEM((5, 96, LANES), F32),
             pltpu.VMEM((PEERS, 96 * LANES), BF16),
             pltpu.VMEM((96, LANES), F32),
             pltpu.VMEM((5 * PEERS, 1024), BF16),
             pltpu.VMEM((256, 1024), BF16),
             pltpu.VMEM((5 * PEERS, 256), F32),
-            pltpu.VMEM((4, SLOT_ROWS, LANES), F32),
+            pltpu.VMEM((4,) + slots, F32),
+            pltpu.VMEM((12,) + slots, F32),
+            pltpu.VMEM((432, 256), F32),
+            pltpu.VMEM((3, 48, 256), F32),
+            pltpu.VMEM((3, 96, LANES), F32),
+            pltpu.VMEM(slots, I32),
+            pltpu.VMEM((192, LANES), F32),
+            messages, messages, messages, messages,
+            pltpu.SemaphoreType.DMA((4,)),
         ],
-        [vmem] * 9,
+        [vmem] * 9 + [smem] + [vmem] * 6,
+        collective_id=0, has_side_effects=True,
     )(
         flat(entry_owner), flat(entry_cell), flat(entry_column), flat(entry_area), flat(area_table),
         tiles_of(profiles), tiles_of(heat_coupling), tiles_of(momentum_coupling), tiles_of(layer_mass),
-    )
-    received = exchange(message)
-    reply, new_soil = call(
-        owner_kernel,
-        [shape((PEERS * MSG_ROWS, LANES), F32), shape((768, LANES), F32)],
-        [
-            pltpu.VMEM((4, SLOT_ROWS, LANES), F32),
-            pltpu.VMEM((9, SLOT_ROWS, LANES), F32),
-            pltpu.VMEM((432, 1024), BF16),
-            pltpu.VMEM((256, 1024), BF16),
-            pltpu.VMEM((432, 256), F32),
-            pltpu.VMEM((3, 48, 256), F32),
-            pltpu.VMEM((3, 96, LANES), F32),
-            pltpu.VMEM((SLOT_ROWS, LANES), I32),
-        ],
-        [smem] + [vmem] * 7,
-    )(
-        layer_counts, received, tiles_of(soil_temps), tiles_of(heat_capacity), tiles_of(conductance),
+        layer_counts, tiles_of(soil_temps), tiles_of(heat_capacity), tiles_of(conductance),
         exchange_coeffs.reshape(3, 96, LANES), flat(wetness), flat(surface_type),
     )
-    returned = exchange(reply)
-    (new_profiles,) = call(
-        column_kernel,
-        [shape((4, 1024, LANES), F32)],
-        [
-            pltpu.VMEM((3, SLOT_ROWS, LANES), F32),
-            pltpu.VMEM((12, SLOT_ROWS, LANES), F32),
-            pltpu.VMEM((192, 1024), BF16),
-            pltpu.VMEM((LANES, 1024), BF16),
-            pltpu.VMEM((192, LANES), F32),
-        ],
-        [vmem] * 7,
-    )(returned, column_slot, weight_slot, wind_slot, factor, reduced, bottom)
     return untile(new_profiles, 64, 2048), untile(new_soil, 8, 12288)
 
 

time: 118 us -> 97.8 us (0.83)
  Pallas kernels: 71.7 us -> 91.5 us
  blocking collectives: 19.3 us -> 0 us
  waiting for transfers between devices: 13 us -> 0 us
  starting transfers between devices: 11.5 us -> 0 us
  local copies, waits for them, and re-layouts: 1.46 us -> 5.53 us
    pallas_call x3 -> x1, Pallas kernels: 71.7 us -> 91.5 us  [local(): call(step_kernel, [shape((4, 1024, LANES), F32), shape((768, LANES), F32)...]
    all_to_all x1 -> x0, blocking collectives: 19.3 us -> none  [exchange(): lax.all_to_all(blocks, ('grp', 'tile'), split_axis=0, concat_axis=0, tile...]
    all_to_all x1 -> x0, waiting for transfers between devices: 13 us -> none  [exchange(): lax.all_to_all(blocks, ('grp', 'tile'), split_axis=0, concat_axis=0, tile...]
    all_to_all x1 -> x0, starting transfers between devices: 11.5 us -> none  [exchange(): lax.all_to_all(blocks, ('grp', 'tile'), split_axis=0, concat_axis=0, tile...]
    unnamed x5, local copies, waits for them, and re-layouts: 1.46 us -> 5.53 us
  transfers between devices with their start and end apart: 1 -> 0, of which waited for: 1 -> 0; matrix products, arithmetic and copies ran while one was open for 1% -> 0% of each run, Pallas kernels for 0% -> 0%
where the time goes in v1:
time: 97.8 us; the launch traced here: 97.7 us
  Pallas kernels  91.5 us (94%)
  local copies, waits for them, and re-layouts  5.53 us (6%)
    pallas_call x1, Pallas kernels, local(): call(step_kernel, [shape((4, 1024, LANES), F32), shape((768, LANES), F32)...  91.5 us
    unnamed x5, local copies, waits for them, and re-layouts  5.53 us

profile of v1, /device:TPU:1, one launch (start us, length us, event | category | flops | bytes accessed | tf_op | source)
XLA Modules:
  0.0 97.7 jit_solution(13305257071174493534)
XLA Ops:
  0.6 1.6 %copy.20 = f32[1,3,96,128]{3,2,1,0:T(8,128)} copy(f32[1,3,96,128]{3,1,2,0:T(4,128)} %bitcast.66) | data formatting | bytes 294912
  2.2 91.5 %shard_map.167 = (f32[4,1024,128]{2,1,0:T(8,128)}, f32[768,128]{1,0:T(8,128)}) custom-call(s32[96,128]{1,0:T(8,128)} %bitcast.67, s32[96,128]{1,0:T(8,128)} %bitcast.68, s32[96,128]{1,0:T(8,128)} %bitcast.69, s32[96,128]{1,0:T(8,128)} %bitcast.70, f32[2,128]{1,0:T(2,128)} %bitcast.73, f32[4,1024,128]{2,1,0:T(8,128)} %bitcast.56, f32[1024,128]{1,0:T(8,128)} %bitcast.59, ...), custom_call_target="tpu_custom_call" | custom-call | tf_op jit(solution)/shard_map/pallas_call | solution.py:540
  93.7 0.0 copy-start
  93.7 3.2 %copy.23 = f32[4,64,2048]{2,1,0:T(8,128)} copy(f32[4,64,2048]{2,1,0:T(8,128)} %bitcast.57) | data formatting | bytes 4194304
  96.9 0.0 copy-done
  96.9 0.7 copy.24
Async XLA Ops:
  93.7 3.2 %copy-start = (f32[768,128]{1,0:T(8,128)S(1)}, f32[768,128]{1,0:T(8,128)}, u32[]{:S(2)}) copy-start(f32[768,128]{1,0:T(8,128)} %get-tuple-element.5) | copy-start | bytes 1179652

commit v2 on v1

v2 whole, which is shorter than its diff:
```python
import jax
import jax.numpy as jnp
from jax import lax
from jax.experimental import pallas as pl
from jax.experimental.pallas import tpu as pltpu
from jax.sharding import PartitionSpec as P

PEERS = 128
LANES = 128
SLOT_ROWS = 192
MSG_ROWS = 8
SEND_ROWS = 6
REPLY_ROWS = 5
CHUNKS = 4
CHUNK_PEERS = PEERS // CHUNKS
LAG = 1
BF16 = jnp.bfloat16
F32 = jnp.float32
I32 = jnp.int32
VMEM_LIMIT = 56 * 1024 * 1024


def iota(shape, dim):
    return lax.broadcasted_iota(I32, shape, dim)


def split3(x):
    high = x.astype(BF16).astype(F32)
    rest = x - high
    mid = rest.astype(BF16).astype(F32)
    return high, mid, rest - mid


def lane_gather(table, index):
    return jnp.take_along_axis(table, index, axis=1, mode="promise_in_bounds")


def dot_nt(a, b):
    return lax.dot_general(a, b, (((1,), (1,)), ((), ())), preferred_element_type=F32)


def low_half(shape):
    return iota(shape, 1) < 64


def aligned(x, step):
    return pl.multiple_of(x * step, step)


def pack_group(j, fields, base, message_ref):
    count = len(fields)
    near_rows = lambda f: pl.ds(aligned(j, 64) + f, 8, stride=8)
    far_rows = lambda f: pl.ds(aligned(j, 64) + 512 + f, 8, stride=8)
    part = lambda f, k: fields[f][pl.ds(base + 8 * k, 8), :]
    for f in range(count):
        message_ref[near_rows(f), :] = part(f, 0)
        message_ref[far_rows(f), :] = part(f, 1)
    for pair in range((count + 1) // 2):
        first = part(2 * pair, 2)
        second = part(2 * pair + 1, 2) if 2 * pair + 1 < count else jnp.zeros_like(first)
        low = low_half(first.shape)
        message_ref[near_rows(count + pair), :] = jnp.where(low, first, pltpu.roll(second, 64, 1))
        message_ref[far_rows(count + pair), :] = jnp.where(low, pltpu.roll(first, 64, 1), second)


def unpack_group(j, message_ref, count):
    near_rows = lambda f: pl.ds(aligned(j, 64) + f, 8, stride=8)
    far_rows = lambda f: pl.ds(aligned(j, 64) + 512 + f, 8, stride=8)
    fields = [[message_ref[near_rows(f), :], message_ref[far_rows(f), :]] for f in range(count)]
    for pair in range((count + 1) // 2):
        near = message_ref[near_rows(count + pair), :]
        far = message_ref[far_rows(count + pair), :]
        low = low_half(near.shape)
        fields[2 * pair].append(jnp.where(low, near, pltpu.roll(far, 64, 1)))
        if 2 * pair + 1 < count:
            fields[2 * pair + 1].append(jnp.where(low, pltpu.roll(near, 64, 1), far))
    return fields


def onehot_rows(ids, count):
    return (iota((count, LANES), 0) == ids).astype(F32).astype(BF16)


def rank_entries(owner_ref, rank_scr):
    upper = (iota((LANES, 2 * LANES), 0) < iota((LANES, 2 * LANES), 1)).astype(F32).astype(BF16)
    owners = iota((PEERS, LANES), 0)
    block = 32

    def body(step, base):
        hits = [owners == owner_ref[pl.ds(step * block + q, 1), :] for q in range(block)]
        onehots = jnp.concatenate([hit.astype(F32).astype(BF16) for hit in hits], axis=0)
        before = jnp.dot(onehots, upper, preferred_element_type=F32)
        for q, hit in enumerate(hits):
            here = before[PEERS * q : PEERS * q + PEERS]
            rank_scr[pl.ds(step * block + q, 1), :] = jnp.sum(
                jnp.where(hit, here[:, :LANES] + base, 0.0), axis=0, keepdims=True
            )
            base = base + here[:, LANES:]
        return base

    lax.fori_loop(0, owner_ref.shape[0] // block, body, jnp.zeros((PEERS, LANES), F32))


def assign_slots(owner_ref, rank_scr, piece_scr, acc_scr):
    acc_scr[...] = jnp.zeros_like(acc_scr)
    ranks = iota((2 * LANES, LANES), 0).astype(F32)
    block = 48

    def body(step, carry):
        lefts, rights = [], []
        for q in range(block):
            r = step * block + q
            onehot = onehot_rows(owner_ref[pl.ds(r, 1), :], PEERS)
            lefts.append(jnp.concatenate([
                onehot * jnp.broadcast_to(piece_scr[p, pl.ds(r, 1), :], (PEERS, LANES)).astype(BF16)
                for p in range(5)
            ], axis=0))
            rights.append((ranks == rank_scr[pl.ds(r, 1), :]).astype(F32).astype(BF16))
        acc_scr[...] += dot_nt(jnp.concatenate(lefts, axis=1), jnp.concatenate(rights, axis=1))
        return carry

    lax.fori_loop(0, owner_ref.shape[0] // block, body, 0)


def down_sweep(profiles_ref, heat_ref, momentum_ref, mass_ref, factor_ref, reduced_ref, bottom_scr):
    couplings = (heat_ref, momentum_ref)
    zero = jnp.zeros((8, LANES), F32)

    def rows_of(g, i, half):
        return pl.ds(g * 128 + half * 64 + i, 8, stride=8)

    def body(g, carry):
        link, factor, reduced, inverse = carry
        link, factor, reduced, inverse = list(link), list(factor), list(reduced), list(inverse)
        following = jnp.minimum(g + 1, 7)
        keep = (g < 7).astype(F32)
        for i in range(8):
            for half in range(2):
                mass = mass_ref[rows_of(g, i, half), :]
                out_rows = pl.ds(pl.multiple_of(g * 128 + i * 16 + half * 8, 8), 8)
                for pair in range(2):
                    k = 2 * pair + half
                    if i < 7:
                        below = couplings[pair][rows_of(g, i + 1, half), :]
                    else:
                        below = couplings[pair][rows_of(following, 0, half), :] * keep
                    here = link[k]
                    divisor = mass + here + below + here * factor[k]
                    inverse[k] = 1.0 / divisor
                    factor[k] = -below * inverse[k]
                    factor_ref[pair, out_rows, :] = factor[k]
                    for member in range(2):
                        field = 2 * pair + member
                        m = 2 * field + half
                        value = profiles_ref[field, rows_of(g, i, half), :]
                        reduced[m] = (mass * value + here * reduced[m]) * inverse[k]
                        reduced_ref[field, out_rows, :] = reduced[m]
                    link[k] = below
        return tuple(link), tuple(factor), tuple(reduced), tuple(inverse)

    first = tuple(couplings[k // 2][rows_of(0, 0, k % 2), :] for k in range(4))
    _, _, reduced, inverse = lax.fori_loop(
        0, 8, body, (first, (zero,) * 4, (zero,) * 8, (zero,) * 4)
    )
    for half in range(2):
        rows = slice(8 * half, 8 * half + 8)
        for field in range(4):
            bottom_scr[field, rows, :] = reduced[2 * field + half]
        bottom_scr[4, rows, :] = inverse[half]
        bottom_scr[5, rows, :] = inverse[2 + half]


def prepare_pieces(cell_ref, column_ref, area_ref, piece_scr):
    cell = cell_ref[...]
    column = column_ref[...]
    piece_scr[0] = ((cell >> 8) + 1).astype(F32)
    piece_scr[1] = (cell & 255).astype(F32)
    piece_scr[2] = (column >> 7).astype(F32)
    piece_scr[3] = (column & 127).astype(F32)
    piece_scr[4] = area_ref[...].astype(F32)


def prepare_group(
    j, acc_scr, table_ref, bottom_ref, field_scr, column_slot_ref, weight_slot_ref, wind_slot_ref, send_scr
):
    near_table = jnp.broadcast_to(table_ref[0:1, :], (8, LANES))
    far_table = jnp.broadcast_to(table_ref[1:2, :], (8, LANES))
    base = aligned(j, 24)

    def pieces(p):
        near = pl.ds(PEERS * p + aligned(j, 8), 8)
        far = pl.ds(PEERS * p + 64 + aligned(j, 8), 8)
        last_near, last_far = acc_scr[near, LANES : 2 * LANES], acc_scr[far, LANES : 2 * LANES]
        last = jnp.where(low_half(last_near.shape), last_near, pltpu.roll(last_far, 64, 1))
        return acc_scr[near, 0:LANES], acc_scr[far, 0:LANES], last

    highs, lows = [], []
    for k, (cell_high, cell_low, row, lane, area) in enumerate(zip(*[pieces(p) for p in range(5)])):
        rows = pl.ds(base + 8 * k, 8)
        field_scr[0, rows, :] = cell_high * 256.0 + cell_low
        row, lane, area = row.astype(I32), lane.astype(I32), area.astype(I32)
        column_slot_ref[rows, :] = row * LANES + lane
        weight = jnp.where(
            area < LANES, lane_gather(near_table, area & 127), lane_gather(far_table, area & 127)
        )
        weight_slot_ref[rows, :] = jnp.where(cell_high > 0.0, weight, 0.0)
        highs.append(row)
        lows.append(lane)
    totals = [[jnp.zeros((8, LANES), F32) for _ in range(4)] for _ in range(3)]
    for h in range(16):
        tables = [jnp.broadcast_to(bottom_ref[f, h : h + 1, :], (8, LANES)) for f in (0, 1, 4, 5)]
        for k in range(3):
            hit = highs[k] == h
            for f in range(4):
                totals[k][f] = jnp.where(hit, lane_gather(tables[f], lows[k]), totals[k][f])
    for k in range(3):
        rows = pl.ds(base + 8 * k, 8)
        for f in range(3):
            field_scr[f + 1, rows, :] = totals[k][f]
        wind_slot_ref[rows, :] = totals[k][3]
    pack_group(j, [field_scr.at[f] for f in range(4)], base, send_scr)


def soil_block(a, b, soil_ref, capacity_ref, conductance_ref, exchange_ref, wetness_ref, type_ref, counts_ref,
               cells_scr, soil_out_ref, table_scr):
    tiles = pl.ds(16 * a + b, 8, stride=2)
    here = (pl.ds(pl.multiple_of(8 * a, 8), 8), slice(LANES * b, LANES * b + LANES))
    bottom_t = cells_scr[0][here]
    bottom_q = cells_scr[1][here]
    heat_scale = cells_scr[2][here]
    kind = type_ref[tiles, :]
    total = jnp.zeros((8, LANES), I32)
    for t in range(4):
        total = jnp.where(kind == t, counts_ref[t], total)
    heat, moist, drag = (exchange_ref[i, tiles, :] for i in range(3))
    gain_t = heat / (1.0 + heat * heat_scale)
    gain_q = moist / (1.0 + moist * heat_scale)
    link_prev = factor = reduced = None
    factors, reduceds = [], []
    for layer in range(8):
        rows = pl.ds((16 * a + b) * 8 + layer, 8, stride=16)
        conductance = conductance_ref[rows, :]
        capacity = capacity_ref[rows, :]
        link = jnp.where(total > layer + 1, conductance, 0.0)
        deep = jnp.where(total == layer + 1, conductance, 0.0)
        diagonal = capacity + link + deep
        rhs = capacity * soil_ref[rows, :]
        if layer == 0:
            divisor = diagonal + gain_t
            rhs = rhs + gain_t * bottom_t
        else:
            divisor = diagonal + link_prev + link_prev * factor
            rhs = rhs + link_prev * reduced
        inverse = 1.0 / divisor
        factor = -link * inverse
        reduced = rhs * inverse
        factors.append(factor)
        reduceds.append(reduced)
        link_prev = link
    value = None
    for layer in range(7, -1, -1):
        rows = pl.ds((16 * a + b) * 8 + layer, 8, stride=16)
        value = reduceds[layer] if layer == 7 else reduceds[layer] - factors[layer] * value
        kept = value if layer == 0 else jnp.where(total > layer, value, soil_ref[rows, :])
        soil_out_ref[rows, :] = kept
    fluxes = (
        gain_t * (value - bottom_t),
        gain_q * (wetness_ref[tiles, :] + 0.5 * value - bottom_q),
        drag,
    )
    for f, flux in enumerate(fluxes):
        table_scr[f, here[0], here[1]] = flux


def clear_cells(acc_scr):
    acc_scr[...] = jnp.zeros_like(acc_scr)


def scatter_group(groups, recv_scr, index_scr, piece_scr, acc_scr):
    lefts, rights = [], []
    for j in groups:
        base = aligned(j, 24)
        ids, *values = unpack_group(j, recv_scr, 4)
        for k in range(3):
            rows = pl.ds(base + 8 * k, 8)
            index_scr[rows, :] = ids[k].astype(I32) - 256
            for f in range(3):
                for p, piece in enumerate(split3(values[f][k])):
                    piece_scr[3 * f + p, rows, :] = piece
        for q in range(24):
            row = pl.ds(base + q, 1)
            cell = index_scr[row, :]
            onehot = onehot_rows(cell >> 8, 48)
            lefts.append(jnp.concatenate([
                onehot * jnp.broadcast_to(piece_scr[p, row, :], (48, LANES)).astype(BF16)
                for p in range(9)
            ], axis=0))
            rights.append(onehot_rows(cell & 255, 256))
    acc_scr[...] += dot_nt(jnp.concatenate(lefts, axis=1), jnp.concatenate(rights, axis=1))


def cells_of_slots(acc_scr, cells_scr):
    for f in range(3):
        base = 144 * f
        cells_scr[f] = (
            acc_scr[base : base + 48] + acc_scr[base + 48 : base + 96] + acc_scr[base + 96 : base + 144]
        )


def solve_soil(*refs):
    def soil_body(a, carry):
        for b in range(2):
            soil_block(a, b, *refs)
        return carry

    lax.fori_loop(0, 6, soil_body, 0)


def cut_table(table_scr, pieces_scr):
    for f in range(3):
        for p, piece in enumerate(split3(table_scr[f])):
            pieces_scr[48 * f : 48 * f + 48, 256 * p : 256 * p + 256] = piece.astype(BF16)


def gather_group(groups, index_scr, pieces_scr, field_scr, reply_scr):
    width = 8 * LANES
    highs, lows = iota((48, width), 0), iota((256, width), 0)
    for j in groups:
        base = aligned(j, 24)
        for k in range(3):
            cell = jnp.concatenate(
                [index_scr[pl.ds(base + 8 * k + q, 1), :] for q in range(8)], axis=1
            )
            onehot = (lows == (cell & 255)).astype(F32).astype(BF16)
            found = sum(
                jnp.dot(pieces_scr[:, 256 * p : 256 * p + 256], onehot, preferred_element_type=F32)
                for p in range(3)
            )
            hit = highs == (cell >> 8)
            for f in range(3):
                value = jnp.sum(
                    jnp.where(hit, found[48 * f : 48 * f + 48], 0.0), axis=0, keepdims=True
                )
                for q in range(8):
                    field_scr[f, pl.ds(base + 8 * k + q, 1), :] = value[:, LANES * q : LANES * q + LANES]
        pack_group(j, [field_scr.at[f] for f in range(3)], base, reply_scr)


def sum_group(groups, return_scr, column_slot_ref, weight_slot_ref, wind_slot_ref, piece_scr, acc_scr):
    lefts, rights = [], []
    for j in groups:
        base = aligned(j, 24)
        heat, moist, drags = unpack_group(j, return_scr, 3)
        for k in range(3):
            rows = pl.ds(base + 8 * k, 8)
            weight = weight_slot_ref[rows, :]
            drag = drags[k]
            values = (
                weight * heat[k],
                weight * moist[k],
                weight * (drag / (1.0 + drag * wind_slot_ref[rows, :])),
                weight,
            )
            for f in range(4):
                for p, piece in enumerate(split3(values[f])):
                    piece_scr[3 * f + p, rows, :] = piece
        for q in range(24):
            row = pl.ds(base + q, 1)
            column = column_slot_ref[row, :]
            onehot = onehot_rows(column >> 7, 16)
            lefts.append(jnp.concatenate([
                onehot * jnp.broadcast_to(piece_scr[p, row, :], (16, LANES)).astype(BF16)
                for p in range(12)
            ], axis=0))
            rights.append(onehot_rows(column & 127, LANES))
    acc_scr[...] += dot_nt(jnp.concatenate(lefts, axis=1), jnp.concatenate(rights, axis=1))


def column_sums(acc_scr):
    sums = []
    for f in range(4):
        base = 48 * f
        sums.append(acc_scr[base : base + 16] + acc_scr[base + 16 : base + 32] + acc_scr[base + 32 : base + 48])
    return sums


def up_sweep(sums, factor_ref, reduced_ref, bottom_ref, out_ref):
    flux = (
        sums[0] / sums[3],
        sums[1] / sums[3],
        -bottom_ref[2] * (sums[2] / sums[3]),
        -bottom_ref[3] * (sums[2] / sums[3]),
    )
    values = []
    for field in range(4):
        lowest = bottom_ref[field] + bottom_ref[4 + field // 2] * flux[field]
        for half in range(2):
            value = lowest[8 * half : 8 * half + 8]
            out_ref[field, pl.ds(7 * 128 + half * 64 + 7, 8, stride=8), :] = value
            values.append(value)

    def retreat(values, g, i):
        values = list(values)
        for half in range(2):
            rows = pl.ds(pl.multiple_of(g * 128 + i * 16 + half * 8, 8), 8)
            for field in range(4):
                k = 2 * field + half
                values[k] = reduced_ref[field, rows, :] - factor_ref[field // 2, rows, :] * values[k]
                out_ref[field, pl.ds(g * 128 + half * 64 + i, 8, stride=8), :] = values[k]
        return tuple(values)

    values = tuple(values)
    for i in range(6, -1, -1):
        values = retreat(values, 7, i)

    def body(step, values):
        for i in range(7, -1, -1):
            values = retreat(values, 6 - step, i)
        return values

    lax.fori_loop(0, 7, body, values)


def device_of(peer):
    return (peer // 32, lax.rem(peer, 32))


def greet(me):
    barrier = pltpu.get_barrier_semaphore()

    def signal(d, carry):
        pl.semaphore_signal(
            barrier, inc=1, device_id=device_of(lax.rem(me + d, PEERS)),
            device_id_type=pl.DeviceIdType.MESH,
        )
        return carry

    lax.fori_loop(1, PEERS, signal, 0)


def send_chunk(me, chunk, own, send_ref, recv_ref, rows, send_sem, recv_sem):
    near = CHUNK_PEERS // 2
    mine = lax.rem(me, near) + near * (me // 64)
    here = pl.ds(aligned(me, MSG_ROWS), rows)
    for k in range(1 if own else 0, CHUNK_PEERS):
        place = lax.rem(mine + k, CHUNK_PEERS) if own else k
        peer = near * chunk + place % near + 64 * (place // near)
        pltpu.make_async_remote_copy(
            src_ref=send_ref.at[pl.ds(aligned(peer, MSG_ROWS), rows)], dst_ref=recv_ref.at[here],
            send_sem=send_sem, recv_sem=recv_sem, device_id=device_of(peer),
            device_id_type=pl.DeviceIdType.MESH,
        ).start()
    if own:
        pltpu.make_async_copy(send_ref.at[here], recv_ref.at[here], recv_sem).start()


def messages_of(me, count, send_ref, recv_ref, rows, send_sem, recv_sem):
    whole = pl.ds(0, count * rows)
    return pltpu.make_async_remote_copy(
        src_ref=send_ref.at[whole], dst_ref=recv_ref.at[whole], send_sem=send_sem, recv_sem=recv_sem,
        device_id=device_of(me), device_id_type=pl.DeviceIdType.MESH,
    )


def step_kernel(
    owner_ref, cell_ref, column_ref, area_ref, table_ref, profiles_ref, heat_ref, momentum_ref, mass_ref,
    counts_ref, soil_ref, capacity_ref, conductance_ref, exchange_ref, wetness_ref, type_ref,
    out_ref, soil_out_ref,
    column_slot_scr, weight_slot_scr, wind_slot_scr, factor_scr, reduced_scr, bottom_scr,
    piece_scr, rank_scr, slot_acc_scr, field_scr, slot_piece_scr, cell_acc_scr, cells_scr, table_scr,
    table_piece_scr, index_scr, column_acc_scr, send_scr, recv_scr, reply_scr, return_scr,
    sent_sem, there_sems, back_sems,
):
    me = lax.axis_index("grp") * 32 + lax.axis_index("tile")
    mine = lax.rem(me, 64) // (CHUNK_PEERS // 2)
    greet(me)
    prepare_pieces(cell_ref, column_ref, area_ref, piece_scr)
    rank_entries(owner_ref, rank_scr)
    assign_slots(owner_ref, rank_scr, piece_scr, slot_acc_scr)
    down_sweep(profiles_ref, heat_ref, momentum_ref, mass_ref, factor_scr, reduced_scr, bottom_scr)
    cell_acc_scr[...] = jnp.zeros_like(cell_acc_scr)
    column_acc_scr[...] = jnp.zeros_like(column_acc_scr)

    def groups_of(chunk):
        return [chunk * (8 // CHUNKS) + k for k in range(8 // CHUNKS)]

    def ahead(i):
        return lax.rem(mine + i, CHUNKS)

    def behind(i):
        return lax.rem(mine + CHUNKS - i, CHUNKS)

    def prepare(i):
        for j in groups_of(ahead(i)):
            prepare_group(
                j, slot_acc_scr, table_ref, bottom_scr, field_scr, column_slot_scr, weight_slot_scr,
                wind_slot_scr, send_scr,
            )

    def send(i, own):
        send_chunk(me, ahead(i), own, send_scr, recv_scr, SEND_ROWS, sent_sem.at[0], there_sems.at[mine])

    def scatter(i):
        chunk = behind(i)
        messages_of(
            me, CHUNK_PEERS, send_scr, recv_scr, SEND_ROWS, sent_sem.at[0], there_sems.at[chunk]
        ).wait_recv()
        scatter_group(groups_of(chunk), recv_scr, index_scr, slot_piece_scr, cell_acc_scr)

    prepare(0)
    pl.semaphore_wait(pltpu.get_barrier_semaphore(), PEERS - 1)
    send(0, True)

    def there(i, carry):
        prepare(i)
        send(i, False)
        scatter(i - 1)
        return carry

    lax.fori_loop(1, CHUNKS, there, 0)
    scatter(CHUNKS - 1)
    cells_of_slots(cell_acc_scr, cells_scr)
    solve_soil(
        soil_ref, capacity_ref, conductance_ref, exchange_ref, wetness_ref, type_ref, counts_ref,
        [cells_scr.at[f] for f in range(3)], soil_out_ref, table_scr,
    )
    cut_table(table_scr, table_piece_scr)

    def gather(i, own):
        chunk = ahead(i)
        gather_group(groups_of(chunk), index_scr, table_piece_scr, field_scr, reply_scr)
        send_chunk(me, chunk, own, reply_scr, return_scr, REPLY_ROWS, sent_sem.at[1], back_sems.at[mine])

    def collect(i):
        chunk = behind(i)
        messages_of(
            me, CHUNK_PEERS, reply_scr, return_scr, REPLY_ROWS, sent_sem.at[1], back_sems.at[chunk]
        ).wait_recv()
        sum_group(
            groups_of(chunk), return_scr, column_slot_scr, weight_slot_scr, wind_slot_scr,
            slot_piece_scr, column_acc_scr,
        )

    gather(0, True)
    for i in range(1, LAG):
        gather(i, False)

    def back(i, carry):
        gather(i, False)
        collect(i - LAG)
        return carry

    lax.fori_loop(LAG, CHUNKS, back, 0)

    def last(i, carry):
        collect(i)
        return carry

    lax.fori_loop(CHUNKS - LAG, CHUNKS, last, 0)
    up_sweep(column_sums(column_acc_scr), factor_scr, reduced_scr, bottom_scr, out_ref)
    messages_of(
        me, PEERS - 1, send_scr, recv_scr, SEND_ROWS, sent_sem.at[0], there_sems.at[0]
    ).wait_send()
    messages_of(
        me, PEERS - 1, reply_scr, return_scr, REPLY_ROWS, sent_sem.at[1], back_sems.at[0]
    ).wait_send()


def call(kernel, out_shapes, scratch, in_specs, **params):
    return pl.pallas_call(
        kernel,
        out_shape=out_shapes,
        in_specs=in_specs,
        out_specs=[pl.BlockSpec(memory_space=pltpu.VMEM)] * len(out_shapes),
        scratch_shapes=scratch,
        compiler_params=pltpu.CompilerParams(vmem_limit_bytes=VMEM_LIMIT, **params),
    )


def tiles_of(x):
    *lead, rows, lanes = x.shape
    x = x.reshape(*lead, rows // 8, 8, lanes // LANES, LANES)
    return jnp.swapaxes(x, -3, -2).reshape(*lead, rows * lanes // LANES, LANES)


def untile(x, rows, lanes):
    *lead, _, _ = x.shape
    x = x.reshape(*lead, rows // 8, lanes // LANES, 8, LANES)
    return jnp.swapaxes(x, -3, -2).reshape(*lead, rows, lanes)


def local(
    profiles, heat_coupling, momentum_coupling, layer_mass, soil_temps, heat_capacity, conductance,
    exchange_coeffs, wetness, area_table, entry_column, entry_owner, entry_cell, entry_area,
    surface_type, layer_counts,
):
    shape = jax.ShapeDtypeStruct
    vmem = pl.BlockSpec(memory_space=pltpu.VMEM)
    smem = pl.BlockSpec(memory_space=pltpu.SMEM)
    flat = lambda x: x.reshape(-1, LANES)
    slots = (SLOT_ROWS, LANES)
    messages = pltpu.VMEM((PEERS * MSG_ROWS, LANES), F32)
    new_profiles, new_soil = call(
        step_kernel,
        [shape((4, 1024, LANES), F32), shape((768, LANES), F32)],
        [
            pltpu.VMEM(slots, I32),
            pltpu.VMEM(slots, F32),
            pltpu.VMEM(slots, F32),
            pltpu.VMEM((2, 1024, LANES), F32),
            pltpu.VMEM((4, 1024, LANES), F32),
            pltpu.VMEM((6, 16, LANES), F32),
            pltpu.VMEM((5, 96, LANES), F32),
            pltpu.VMEM((96, LANES), F32),
            pltpu.VMEM((5 * PEERS, 256), F32),
            pltpu.VMEM((4,) + slots, F32),
            pltpu.VMEM((12,) + slots, F32),
            pltpu.VMEM((432, 256), F32),
            pltpu.VMEM((3, 48, 256), F32),
            pltpu.VMEM((3, 48, 256), F32),
            pltpu.VMEM((144, 768), BF16),
            pltpu.VMEM(slots, I32),
            pltpu.VMEM((192, LANES), F32),
            messages, messages, messages, messages,
            pltpu.SemaphoreType.DMA((2,)),
            pltpu.SemaphoreType.DMA((CHUNKS,)),
            pltpu.SemaphoreType.DMA((CHUNKS,)),
        ],
        [vmem] * 9 + [smem] + [vmem] * 6,
        collective_id=0, has_side_effects=True,
    )(
        flat(entry_owner), flat(entry_cell), flat(entry_column), flat(entry_area), flat(area_table),
        tiles_of(profiles), tiles_of(heat_coupling), tiles_of(momentum_coupling), tiles_of(layer_mass),
        layer_counts, tiles_of(soil_temps), tiles_of(heat_capacity), tiles_of(conductance),
        exchange_coeffs.reshape(3, 96, LANES), flat(wetness), flat(surface_type),
    )
    return untile(new_profiles, 64, 2048), untile(new_soil, 8, 12288)


def solution(mesh):
    split = ("grp", "tile")
    return jax.shard_map(
        local,
        mesh=mesh,
        in_specs=(
            P(None, None, split), P(None, split), P(None, split), P(None, split), P(None, split),
            P(None, split), P(None, split), P(None, split), P(split), P(), P(split), P(split),
            P(split), P(split), P(split), P(),
        ),
        out_specs=(P(None, None, split), P(None, split)),
        check_vma=False,
    )
```

time: 97.8 us -> 69 us (0.71)
  Pallas kernels: 91.5 us -> 62.6 us
    pallas_call x1, Pallas kernels: 91.5 us -> 62.6 us  [local(): call(step_kernel, [shape((4, 1024, LANES), F32), shape((768, LANES), F32)...]
where the time goes in v2:
time: 69 us; the launch traced here: 68.8 us
  Pallas kernels  62.6 us (91%)
  local copies, waits for them, and re-layouts  5.53 us (8%)
    pallas_call x1, Pallas kernels, local(): call(step_kernel, [shape((4, 1024, LANES), F32), shape((768, LANES), F32)...  62.6 us
    unnamed x5, local copies, waits for them, and re-layouts  5.53 us

profile of v2, /device:TPU:1, one launch (start us, length us, event | category | flops | bytes accessed | tf_op | source)
XLA Modules:
  0.0 68.8 jit_solution(5892513841331121825)
XLA Ops:
  0.6 1.6 %copy.20 = f32[1,3,96,128]{3,2,1,0:T(8,128)} copy(f32[1,3,96,128]{3,1,2,0:T(4,128)} %bitcast.66) | data formatting | bytes 294912
  2.2 62.6 %shard_map.167 = (f32[4,1024,128]{2,1,0:T(8,128)}, f32[768,128]{1,0:T(8,128)}) custom-call(s32[96,128]{1,0:T(8,128)} %bitcast.67, s32[96,128]{1,0:T(8,128)} %bitcast.68, s32[96,128]{1,0:T(8,128)} %bitcast.69, s32[96,128]{1,0:T(8,128)} %bitcast.70, f32[2,128]{1,0:T(2,128)} %bitcast.73, f32[4,1024,128]{2,1,0:T(8,128)} %bitcast.56, f32[1024,128]{1,0:T(8,128)} %bitcast.59, ...), custom_call_target="tpu_custom_call" | custom-call | tf_op jit(solution)/shard_map/pallas_call | solution.py:603
  64.9 0.0 copy-start
  64.9 3.2 %copy.23 = f32[4,64,2048]{2,1,0:T(8,128)} copy(f32[4,64,2048]{2,1,0:T(8,128)} %bitcast.57) | data formatting | bytes 4194304
  68.1 0.0 copy-done
  68.1 0.7 %copy.24 = f32[8,12288]{1,0:T(8,128)} copy(f32[8,12288]{1,0:T(8,128)S(1)} %bitcast.65) | data formatting | bytes 786432
Async XLA Ops:
  64.9 3.2 %copy-start = (f32[768,128]{1,0:T(8,128)S(1)}, f32[768,128]{1,0:T(8,128)}, u32[]{:S(2)}) copy-start(f32[768,128]{1,0:T(8,128)} %get-tuple-element.5) | copy-start | bytes 1179652

commit v3 on v2

--- a/solution.py
+++ b/solution.py
@@ -13,7 +13,8 @@
 REPLY_ROWS = 5
 CHUNKS = 4
 CHUNK_PEERS = PEERS // CHUNKS
-LAG = 1
+LAG = 3
+PIECES = 2
 BF16 = jnp.bfloat16
 F32 = jnp.float32
 I32 = jnp.int32
@@ -24,11 +25,12 @@
     return lax.broadcasted_iota(I32, shape, dim)
 
 
-def split3(x):
-    high = x.astype(BF16).astype(F32)
-    rest = x - high
-    mid = rest.astype(BF16).astype(F32)
-    return high, mid, rest - mid
+def split(x):
+    pieces = []
+    for _ in range(PIECES):
+        pieces.append(x.astype(BF16).astype(F32))
+        x = x - pieces[-1]
+    return pieces
 
 
 def lane_gather(table, index):
@@ -81,12 +83,13 @@
     return (iota((count, LANES), 0) == ids).astype(F32).astype(BF16)
 
 
-def rank_entries(owner_ref, rank_scr):
+def rank_entries(owner_ref, rank_scr, greet):
     upper = (iota((LANES, 2 * LANES), 0) < iota((LANES, 2 * LANES), 1)).astype(F32).astype(BF16)
     owners = iota((PEERS, LANES), 0)
     block = 32
 
     def body(step, base):
+        greet(step)
         hits = [owners == owner_ref[pl.ds(step * block + q, 1), :] for q in range(block)]
         onehots = jnp.concatenate([hit.astype(F32).astype(BF16) for hit in hits], axis=0)
         before = jnp.dot(onehots, upper, preferred_element_type=F32)
@@ -285,15 +288,15 @@
             rows = pl.ds(base + 8 * k, 8)
             index_scr[rows, :] = ids[k].astype(I32) - 256
             for f in range(3):
-                for p, piece in enumerate(split3(values[f][k])):
-                    piece_scr[3 * f + p, rows, :] = piece
+                for p, piece in enumerate(split(values[f][k])):
+                    piece_scr[PIECES * f + p, rows, :] = piece
         for q in range(24):
             row = pl.ds(base + q, 1)
             cell = index_scr[row, :]
             onehot = onehot_rows(cell >> 8, 48)
             lefts.append(jnp.concatenate([
                 onehot * jnp.broadcast_to(piece_scr[p, row, :], (48, LANES)).astype(BF16)
-                for p in range(9)
+                for p in range(3 * PIECES)
             ], axis=0))
             rights.append(onehot_rows(cell & 255, 256))
     acc_scr[...] += dot_nt(jnp.concatenate(lefts, axis=1), jnp.concatenate(rights, axis=1))
@@ -301,10 +304,8 @@
 
 def cells_of_slots(acc_scr, cells_scr):
     for f in range(3):
-        base = 144 * f
-        cells_scr[f] = (
-            acc_scr[base : base + 48] + acc_scr[base + 48 : base + 96] + acc_scr[base + 96 : base + 144]
-        )
+        base = 48 * PIECES * f
+        cells_scr[f] = sum(acc_scr[base + 48 * p : base + 48 * p + 48] for p in range(PIECES))
 
 
 def solve_soil(*refs):
@@ -318,7 +319,7 @@
 
 def cut_table(table_scr, pieces_scr):
     for f in range(3):
-        for p, piece in enumerate(split3(table_scr[f])):
+        for p, piece in enumerate(split(table_scr[f])):
             pieces_scr[48 * f : 48 * f + 48, 256 * p : 256 * p + 256] = piece.astype(BF16)
 
 
@@ -334,7 +335,7 @@
             onehot = (lows == (cell & 255)).astype(F32).astype(BF16)
             found = sum(
                 jnp.dot(pieces_scr[:, 256 * p : 256 * p + 256], onehot, preferred_element_type=F32)
-                for p in range(3)
+                for p in range(PIECES)
             )
             hit = highs == (cell >> 8)
             for f in range(3):
@@ -362,15 +363,15 @@
                 weight,
             )
             for f in range(4):
-                for p, piece in enumerate(split3(values[f])):
-                    piece_scr[3 * f + p, rows, :] = piece
+                for p, piece in enumerate(split(values[f])):
+                    piece_scr[PIECES * f + p, rows, :] = piece
         for q in range(24):
             row = pl.ds(base + q, 1)
             column = column_slot_ref[row, :]
             onehot = onehot_rows(column >> 7, 16)
             lefts.append(jnp.concatenate([
                 onehot * jnp.broadcast_to(piece_scr[p, row, :], (16, LANES)).astype(BF16)
-                for p in range(12)
+                for p in range(4 * PIECES)
             ], axis=0))
             rights.append(onehot_rows(column & 127, LANES))
     acc_scr[...] += dot_nt(jnp.concatenate(lefts, axis=1), jnp.concatenate(rights, axis=1))
@@ -379,63 +380,75 @@
 def column_sums(acc_scr):
     sums = []
     for f in range(4):
-        base = 48 * f
-        sums.append(acc_scr[base : base + 16] + acc_scr[base + 16 : base + 32] + acc_scr[base + 32 : base + 48])
+        base = 16 * PIECES * f
+        sums.append(sum(acc_scr[base + 16 * p : base + 16 * p + 16] for p in range(PIECES)))
     return sums
 
 
-def up_sweep(sums, factor_ref, reduced_ref, bottom_ref, out_ref):
+def lowest_values(sums, bottom_ref, lowest_ref):
     flux = (
         sums[0] / sums[3],
         sums[1] / sums[3],
         -bottom_ref[2] * (sums[2] / sums[3]),
         -bottom_ref[3] * (sums[2] / sums[3]),
     )
-    values = []
     for field in range(4):
-        lowest = bottom_ref[field] + bottom_ref[4 + field // 2] * flux[field]
-        for half in range(2):
-            value = lowest[8 * half : 8 * half + 8]
-            out_ref[field, pl.ds(7 * 128 + half * 64 + 7, 8, stride=8), :] = value
-            values.append(value)
-
-    def retreat(values, g, i):
-        values = list(values)
-        for half in range(2):
-            rows = pl.ds(pl.multiple_of(g * 128 + i * 16 + half * 8, 8), 8)
-            for field in range(4):
-                k = 2 * field + half
-                values[k] = reduced_ref[field, rows, :] - factor_ref[field // 2, rows, :] * values[k]
-                out_ref[field, pl.ds(g * 128 + half * 64 + i, 8, stride=8), :] = values[k]
-        return tuple(values)
-
-    values = tuple(values)
-    for i in range(6, -1, -1):
-        values = retreat(values, 7, i)
-
-    def body(step, values):
+        lowest_ref[field] = bottom_ref[field] + bottom_ref[4 + field // 2] * flux[field]
+
+
+def up_kernel(
+    lowest_ref, factor_ref, reduced_ref, soil_ref, out_ref, soil_out_ref,
+    factor_scr, reduced_scr, out_scr, soil_scr, soil_sems, factor_sems, reduced_sems, out_sems,
+):
+    soil_load = pltpu.make_async_copy(soil_ref, soil_scr, soil_sems.at[0])
+    soil_store = pltpu.make_async_copy(soil_scr, soil_out_ref, soil_sems.at[1])
+
+    def part(source, target, sems, g):
+        rows = pl.ds(128 * g, 128)
+        return pltpu.make_async_copy(source.at[:, rows], target.at[:, rows], sems.at[g])
+
+    loads = [
+        (part(factor_ref, factor_scr, factor_sems, g), part(reduced_ref, reduced_scr, reduced_sems, g))
+        for g in range(8)
+    ]
+    stores = [part(out_scr, out_ref, out_sems, g) for g in range(8)]
+    for g in range(7, -1, -1):
+        for load in loads[g]:
+            load.start()
+    soil_load.start()
+    values = [lowest_ref[field, 8 * half : 8 * half + 8] for field in range(4) for half in range(2)]
+    for g in range(7, -1, -1):
+        for load in loads[g]:
+            load.wait()
         for i in range(7, -1, -1):
-            values = retreat(values, 6 - step, i)
-        return values
-
-    lax.fori_loop(0, 7, body, values)
+            for half in range(2):
+                rows = pl.ds(g * 128 + i * 16 + half * 8, 8)
+                for field in range(4):
+                    k = 2 * field + half
+                    if g < 7 or i < 7:
+                        factor = factor_scr[field // 2, rows, :]
+                        values[k] = reduced_scr[field, rows, :] - factor * values[k]
+                    out_scr[field, pl.ds(g * 128 + half * 64 + i, 8, stride=8), :] = values[k]
+        stores[g].start()
+        if g == 4:
+            soil_load.wait()
+            soil_store.start()
+    for store in stores:
+        store.wait()
+    soil_store.wait()
 
 
 def device_of(peer):
     return (peer // 32, lax.rem(peer, 32))
 
 
-def greet(me):
+def greet(me, first, count):
     barrier = pltpu.get_barrier_semaphore()
-
-    def signal(d, carry):
+    for k in range(count):
         pl.semaphore_signal(
-            barrier, inc=1, device_id=device_of(lax.rem(me + d, PEERS)),
+            barrier, inc=1, device_id=device_of(lax.rem(me + first + k, PEERS)),
             device_id_type=pl.DeviceIdType.MESH,
         )
-        return carry
-
-    lax.fori_loop(1, PEERS, signal, 0)
 
 
 def send_chunk(me, chunk, own, send_ref, recv_ref, rows, send_sem, recv_sem):
@@ -443,7 +456,7 @@
     mine = lax.rem(me, near) + near * (me // 64)
     here = pl.ds(aligned(me, MSG_ROWS), rows)
     for k in range(1 if own else 0, CHUNK_PEERS):
-        place = lax.rem(mine + k, CHUNK_PEERS) if own else k
+        place = lax.rem(mine + k, CHUNK_PEERS)
         peer = near * chunk + place % near + 64 * (place // near)
         pltpu.make_async_remote_copy(
             src_ref=send_ref.at[pl.ds(aligned(peer, MSG_ROWS), rows)], dst_ref=recv_ref.at[here],
@@ -463,9 +476,10 @@
 
 
 def step_kernel(
-    owner_ref, cell_ref, column_ref, area_ref, table_ref, profiles_ref, heat_ref, momentum_ref, mass_ref,
-    counts_ref, soil_ref, capacity_ref, conductance_ref, exchange_ref, wetness_ref, type_ref,
-    out_ref, soil_out_ref,
+    owner_ref, cell_ref, column_ref, area_ref, table_ref, profiles_any, heat_any, momentum_any, mass_any,
+    counts_ref, soil_any, capacity_any, conductance_any, exchange_ref, wetness_ref, type_ref,
+    lowest_ref, soil_out_ref, factor_any, reduced_any,
+    profiles_ref, heat_ref, momentum_ref, mass_ref, soil_ref, capacity_ref, conductance_ref, load_sems,
     column_slot_scr, weight_slot_scr, wind_slot_scr, factor_scr, reduced_scr, bottom_scr,
     piece_scr, rank_scr, slot_acc_scr, field_scr, slot_piece_scr, cell_acc_scr, cells_scr, table_scr,
     table_piece_scr, index_scr, column_acc_scr, send_scr, recv_scr, reply_scr, return_scr,
@@ -473,11 +487,34 @@
 ):
     me = lax.axis_index("grp") * 32 + lax.axis_index("tile")
     mine = lax.rem(me, 64) // (CHUNK_PEERS // 2)
-    greet(me)
+    column_loads = [
+        pltpu.make_async_copy(source, target, load_sems.at[k])
+        for k, (source, target) in enumerate((
+            (heat_any, heat_ref), (momentum_any, momentum_ref), (mass_any, mass_ref),
+            (profiles_any, profiles_ref),
+        ))
+    ]
+    soil_loads = [
+        pltpu.make_async_copy(source, target, load_sems.at[4 + k])
+        for k, (source, target) in enumerate((
+            (soil_any, soil_ref), (capacity_any, capacity_ref), (conductance_any, conductance_ref),
+        ))
+    ]
+    sweep_stores = [
+        pltpu.make_async_copy(factor_scr, factor_any, load_sems.at[7]),
+        pltpu.make_async_copy(reduced_scr, reduced_any, load_sems.at[8]),
+    ]
+    for load in column_loads + soil_loads:
+        load.start()
+    greet(me, 1, 1)
     prepare_pieces(cell_ref, column_ref, area_ref, piece_scr)
-    rank_entries(owner_ref, rank_scr)
+    rank_entries(owner_ref, rank_scr, lambda step: greet(me, 2 + 42 * step, 42))
     assign_slots(owner_ref, rank_scr, piece_scr, slot_acc_scr)
+    for load in column_loads:
+        load.wait()
     down_sweep(profiles_ref, heat_ref, momentum_ref, mass_ref, factor_scr, reduced_scr, bottom_scr)
+    for store in sweep_stores:
+        store.start()
     cell_acc_scr[...] = jnp.zeros_like(cell_acc_scr)
     column_acc_scr[...] = jnp.zeros_like(column_acc_scr)
 
@@ -514,11 +551,17 @@
     def there(i, carry):
         prepare(i)
         send(i, False)
-        scatter(i - 1)
         return carry
 
     lax.fori_loop(1, CHUNKS, there, 0)
-    scatter(CHUNKS - 1)
+
+    def arrive(i, carry):
+        scatter(i)
+        return carry
+
+    lax.fori_loop(0, CHUNKS, arrive, 0)
+    for load in soil_loads:
+        load.wait()
     cells_of_slots(cell_acc_scr, cells_scr)
     solve_soil(
         soil_ref, capacity_ref, conductance_ref, exchange_ref, wetness_ref, type_ref, counts_ref,
@@ -542,22 +585,29 @@
         )
 
     gather(0, True)
-    for i in range(1, LAG):
+
+    def ask(i, carry):
         gather(i, False)
+        return carry
+
+    lax.fori_loop(1, LAG, ask, 0)
 
     def back(i, carry):
         gather(i, False)
         collect(i - LAG)
         return carry
 
-    lax.fori_loop(LAG, CHUNKS, back, 0)
+    if LAG < CHUNKS:
+        lax.fori_loop(LAG, CHUNKS, back, 0)
 
     def last(i, carry):
         collect(i)
         return carry
 
     lax.fori_loop(CHUNKS - LAG, CHUNKS, last, 0)
-    up_sweep(column_sums(column_acc_scr), factor_scr, reduced_scr, bottom_scr, out_ref)
+    lowest_values(column_sums(column_acc_scr), bottom_scr, lowest_ref)
+    for store in sweep_stores:
+        store.wait()
     messages_of(
         me, PEERS - 1, send_scr, recv_scr, SEND_ROWS, sent_sem.at[0], there_sems.at[0]
     ).wait_send()
@@ -566,12 +616,12 @@
     ).wait_send()
 
 
-def call(kernel, out_shapes, scratch, in_specs, **params):
+def call(kernel, out_shapes, scratch, in_specs, out_specs, **params):
     return pl.pallas_call(
         kernel,
         out_shape=out_shapes,
         in_specs=in_specs,
-        out_specs=[pl.BlockSpec(memory_space=pltpu.VMEM)] * len(out_shapes),
+        out_specs=out_specs,
         scratch_shapes=scratch,
         compiler_params=pltpu.CompilerParams(vmem_limit_bytes=VMEM_LIMIT, **params),
     )
@@ -600,10 +650,18 @@
     flat = lambda x: x.reshape(-1, LANES)
     slots = (SLOT_ROWS, LANES)
     messages = pltpu.VMEM((PEERS * MSG_ROWS, LANES), F32)
-    new_profiles, new_soil = call(
+    anywhere = pl.BlockSpec(memory_space=pl.ANY)
+    columns, cells = pltpu.VMEM((1024, LANES), F32), pltpu.VMEM((768, LANES), F32)
+    lowest, soil, factor, reduced = call(
         step_kernel,
-        [shape((4, 1024, LANES), F32), shape((768, LANES), F32)],
         [
+            shape((4, 16, LANES), F32), shape((768, LANES), F32),
+            shape((2, 1024, LANES), F32), shape((4, 1024, LANES), F32),
+        ],
+        [
+            pltpu.VMEM((4, 1024, LANES), F32),
+            columns, columns, columns, cells, cells, cells,
+            pltpu.SemaphoreType.DMA((9,)),
             pltpu.VMEM(slots, I32),
             pltpu.VMEM(slots, F32),
             pltpu.VMEM(slots, F32),
@@ -614,19 +672,20 @@
             pltpu.VMEM((96, LANES), F32),
             pltpu.VMEM((5 * PEERS, 256), F32),
             pltpu.VMEM((4,) + slots, F32),
-            pltpu.VMEM((12,) + slots, F32),
-            pltpu.VMEM((432, 256), F32),
+            pltpu.VMEM((4 * PIECES,) + slots, F32),
+            pltpu.VMEM((144 * PIECES, 256), F32),
             pltpu.VMEM((3, 48, 256), F32),
             pltpu.VMEM((3, 48, 256), F32),
-            pltpu.VMEM((144, 768), BF16),
+            pltpu.VMEM((144, 256 * PIECES), BF16),
             pltpu.VMEM(slots, I32),
-            pltpu.VMEM((192, LANES), F32),
+            pltpu.VMEM((64 * PIECES, LANES), F32),
             messages, messages, messages, messages,
             pltpu.SemaphoreType.DMA((2,)),
             pltpu.SemaphoreType.DMA((CHUNKS,)),
             pltpu.SemaphoreType.DMA((CHUNKS,)),
         ],
-        [vmem] * 9 + [smem] + [vmem] * 6,
+        [vmem] * 5 + [anywhere] * 4 + [smem] + [anywhere] * 3 + [vmem] * 3,
+        [vmem] * 2 + [anywhere] * 2,
         collective_id=0, has_side_effects=True,
     )(
         flat(entry_owner), flat(entry_cell), flat(entry_column), flat(entry_area), flat(area_table),
@@ -634,6 +693,22 @@
         layer_counts, tiles_of(soil_temps), tiles_of(heat_capacity), tiles_of(conductance),
         exchange_coeffs.reshape(3, 96, LANES), flat(wetness), flat(surface_type),
     )
+    new_profiles, new_soil = call(
+        up_kernel,
+        [shape((4, 1024, LANES), F32), shape((768, LANES), F32)],
+        [
+            pltpu.VMEM((2, 1024, LANES), F32),
+            pltpu.VMEM((4, 1024, LANES), F32),
+            pltpu.VMEM((4, 1024, LANES), F32),
+            cells,
+            pltpu.SemaphoreType.DMA((2,)),
+            pltpu.SemaphoreType.DMA((8,)),
+            pltpu.SemaphoreType.DMA((8,)),
+            pltpu.SemaphoreType.DMA((8,)),
+        ],
+        [vmem] + [anywhere] * 3,
+        [anywhere] * 2,
+    )(lowest, factor, reduced, soil)
     return untile(new_profiles, 64, 2048), untile(new_soil, 8, 12288)
 
 

time: 69 us -> 50.6 us (0.73)
  Pallas kernels: 62.6 us -> 47.9 us
  local copies, waits for them, and re-layouts: 5.53 us -> 1.6 us
    pallas_call x1 -> x2, Pallas kernels: 62.6 us -> 47.9 us  [the longest x1 43.8 us: local(): call(step_kernel, [shape((4, 16, LANES), F32), shape((768, LANES), F32),...]
    unnamed x5 -> x1, local copies, waits for them, and re-layouts: 5.53 us -> 1.6 us
where the time goes in v3:
time: 50.6 us; the launch traced here: 50.3 us
  Pallas kernels  47.9 us (95%)
  local copies, waits for them, and re-layouts  1.6 us (3%)
  between operations  0.8 us (2%)
    pallas_call x1, Pallas kernels, local(): call(step_kernel, [shape((4, 16, LANES), F32), shape((768, LANES), F32),...  43.8 us
    pallas_call x1, Pallas kernels, local(): call(up_kernel, [shape((4, 1024, LANES), F32), shape((768, LANES), F32)],...  4.11 us
    unnamed x1, local copies, waits for them, and re-layouts  1.6 us

profile of v3, /device:TPU:1, one launch (start us, length us, event | category | flops | bytes accessed | tf_op | source)
XLA Modules:
  0.0 50.3 jit_solution(7428543485203174591)
XLA Ops:
  0.6 1.6 %copy.20 = f32[1,3,96,128]{3,2,1,0:T(8,128)} copy(f32[1,3,96,128]{3,1,2,0:T(4,128)} %bitcast.64) | data formatting | bytes 294912
  2.2 43.8 %shard_map.167 = (f32[4,16,128]{2,1,0:T(8,128)}, f32[768,128]{1,0:T(8,128)}, f32[2,1024,128]{2,1,0:T(8,128)}, f32[4,1024,128]{2,1,0:T(8,128)}) custom-call(s32[96,128]{1,0:T(8,128)} %bitcast.65, s32[96,128]{1,0:T(8,128)} %bitcast.66, s32[96,128]{1,0:T(8,128)} %bitcast.67, s32[96,128]{1,0:T(8,128)} %bitcast.68, f32[2,128]{1,0:T(2,128)} %bitcast.71, ...), custom_call_target="tpu_custom_call" | custom-call | tf_op jit(solution)/shard_map/pallas_call | solution.py:655
  46.1 4.1 %shard_map.168 = (f32[4,1024,128]{2,1,0:T(8,128)}, f32[768,128]{1,0:T(8,128)}) custom-call(f32[4,16,128]{2,1,0:T(8,128)} %get-tuple-element.8.lowest_ref, f32[2,1024,128]{2,1,0:T(8,128)} %get-tuple-element.9.factor_ref, f32[4,1024,128]{2,1,0:T(8,128)} %get-tuple-element.10.reduced_ref, f32[768,128]{1,0:T(8,128)} %get-tuple-element.11.soil_ref), custom_call_target="tpu_custom_call" | custom-call | tf_op jit(solution)/shard_map/pallas_call | solution.py:696

commit v4 on v3

--- a/solution.py
+++ b/solution.py
@@ -18,7 +18,7 @@
 BF16 = jnp.bfloat16
 F32 = jnp.float32
 I32 = jnp.int32
-VMEM_LIMIT = 56 * 1024 * 1024
+VMEM_LIMIT = 28 * 1024 * 1024
 
 
 def iota(shape, dim):
@@ -396,46 +396,30 @@
         lowest_ref[field] = bottom_ref[field] + bottom_ref[4 + field // 2] * flux[field]
 
 
-def up_kernel(
-    lowest_ref, factor_ref, reduced_ref, soil_ref, out_ref, soil_out_ref,
-    factor_scr, reduced_scr, out_scr, soil_scr, soil_sems, factor_sems, reduced_sems, out_sems,
-):
-    soil_load = pltpu.make_async_copy(soil_ref, soil_scr, soil_sems.at[0])
-    soil_store = pltpu.make_async_copy(soil_scr, soil_out_ref, soil_sems.at[1])
-
-    def part(source, target, sems, g):
-        rows = pl.ds(128 * g, 128)
-        return pltpu.make_async_copy(source.at[:, rows], target.at[:, rows], sems.at[g])
-
-    loads = [
-        (part(factor_ref, factor_scr, factor_sems, g), part(reduced_ref, reduced_scr, reduced_sems, g))
+def up_kernel(lowest_ref, factor_ref, reduced_ref, soil_ref, out_ref, soil_out_ref, out_scr, soil_sem, out_sems):
+    soil = pltpu.make_async_copy(soil_ref, soil_out_ref, soil_sem)
+    soil.start()
+    stores = [
+        pltpu.make_async_copy(
+            out_scr.at[:, pl.ds(128 * g, 128)], out_ref.at[:, pl.ds(128 * g, 128)], out_sems.at[g]
+        )
         for g in range(8)
     ]
-    stores = [part(out_scr, out_ref, out_sems, g) for g in range(8)]
-    for g in range(7, -1, -1):
-        for load in loads[g]:
-            load.start()
-    soil_load.start()
     values = [lowest_ref[field, 8 * half : 8 * half + 8] for field in range(4) for half in range(2)]
     for g in range(7, -1, -1):
-        for load in loads[g]:
-            load.wait()
         for i in range(7, -1, -1):
             for half in range(2):
                 rows = pl.ds(g * 128 + i * 16 + half * 8, 8)
                 for field in range(4):
                     k = 2 * field + half
                     if g < 7 or i < 7:
-                        factor = factor_scr[field // 2, rows, :]
-                        values[k] = reduced_scr[field, rows, :] - factor * values[k]
+                        factor = factor_ref[field // 2, rows, :]
+                        values[k] = reduced_ref[field, rows, :] - factor * values[k]
                     out_scr[field, pl.ds(g * 128 + half * 64 + i, 8, stride=8), :] = values[k]
         stores[g].start()
-        if g == 4:
-            soil_load.wait()
-            soil_store.start()
     for store in stores:
         store.wait()
-    soil_store.wait()
+    soil.wait()
 
 
 def device_of(peer):
@@ -476,45 +460,43 @@
 
 
 def step_kernel(
-    owner_ref, cell_ref, column_ref, area_ref, table_ref, profiles_any, heat_any, momentum_any, mass_any,
-    counts_ref, soil_any, capacity_any, conductance_any, exchange_ref, wetness_ref, type_ref,
-    lowest_ref, soil_out_ref, factor_any, reduced_any,
+    owner_any, cell_any, column_any, area_any, table_any, profiles_any, heat_any, momentum_any, mass_any,
+    counts_ref, soil_any, capacity_any, conductance_any, exchange_any, wetness_any, type_any,
+    lowest_ref, soil_out_ref, factor_scr, reduced_scr,
+    owner_ref, cell_ref, column_ref, area_ref, table_ref, exchange_ref, wetness_ref, type_ref,
     profiles_ref, heat_ref, momentum_ref, mass_ref, soil_ref, capacity_ref, conductance_ref, load_sems,
-    column_slot_scr, weight_slot_scr, wind_slot_scr, factor_scr, reduced_scr, bottom_scr,
+    exchange_scr,
+    column_slot_scr, weight_slot_scr, wind_slot_scr, bottom_scr,
     piece_scr, rank_scr, slot_acc_scr, field_scr, slot_piece_scr, cell_acc_scr, cells_scr, table_scr,
     table_piece_scr, index_scr, column_acc_scr, send_scr, recv_scr, reply_scr, return_scr,
     sent_sem, there_sems, back_sems,
 ):
     me = lax.axis_index("grp") * 32 + lax.axis_index("tile")
     mine = lax.rem(me, 64) // (CHUNK_PEERS // 2)
-    column_loads = [
+    loads = [
         pltpu.make_async_copy(source, target, load_sems.at[k])
         for k, (source, target) in enumerate((
-            (heat_any, heat_ref), (momentum_any, momentum_ref), (mass_any, mass_ref),
-            (profiles_any, profiles_ref),
+            (owner_any, owner_ref), (cell_any, cell_ref), (column_any, column_ref), (area_any, area_ref),
+            (table_any, table_ref), (heat_any, heat_ref), (momentum_any, momentum_ref),
+            (mass_any, mass_ref), (profiles_any, profiles_ref), (exchange_any, exchange_ref),
+            (soil_any, soil_ref), (capacity_any, capacity_ref), (conductance_any, conductance_ref),
+            (wetness_any, wetness_ref), (type_any, type_ref),
         ))
     ]
-    soil_loads = [
-        pltpu.make_async_copy(source, target, load_sems.at[4 + k])
-        for k, (source, target) in enumerate((
-            (soil_any, soil_ref), (capacity_any, capacity_ref), (conductance_any, conductance_ref),
-        ))
-    ]
-    sweep_stores = [
-        pltpu.make_async_copy(factor_scr, factor_any, load_sems.at[7]),
-        pltpu.make_async_copy(reduced_scr, reduced_any, load_sems.at[8]),
-    ]
-    for load in column_loads + soil_loads:
+    entry_loads, column_loads, soil_loads = loads[:4], loads[4:10], loads[10:]
+    for load in loads:
         load.start()
     greet(me, 1, 1)
+    for load in entry_loads:
+        load.wait()
     prepare_pieces(cell_ref, column_ref, area_ref, piece_scr)
     rank_entries(owner_ref, rank_scr, lambda step: greet(me, 2 + 42 * step, 42))
     assign_slots(owner_ref, rank_scr, piece_scr, slot_acc_scr)
     for load in column_loads:
         load.wait()
+    for row in range(3):
+        exchange_scr[row] = exchange_ref[row : row + 1, :].reshape(96, LANES)
     down_sweep(profiles_ref, heat_ref, momentum_ref, mass_ref, factor_scr, reduced_scr, bottom_scr)
-    for store in sweep_stores:
-        store.start()
     cell_acc_scr[...] = jnp.zeros_like(cell_acc_scr)
     column_acc_scr[...] = jnp.zeros_like(column_acc_scr)
 
@@ -564,7 +546,7 @@
         load.wait()
     cells_of_slots(cell_acc_scr, cells_scr)
     solve_soil(
-        soil_ref, capacity_ref, conductance_ref, exchange_ref, wetness_ref, type_ref, counts_ref,
+        soil_ref, capacity_ref, conductance_ref, exchange_scr, wetness_ref, type_ref, counts_ref,
         [cells_scr.at[f] for f in range(3)], soil_out_ref, table_scr,
     )
     cut_table(table_scr, table_piece_scr)
@@ -606,8 +588,6 @@
 
     lax.fori_loop(CHUNKS - LAG, CHUNKS, last, 0)
     lowest_values(column_sums(column_acc_scr), bottom_scr, lowest_ref)
-    for store in sweep_stores:
-        store.wait()
     messages_of(
         me, PEERS - 1, send_scr, recv_scr, SEND_ROWS, sent_sem.at[0], there_sems.at[0]
     ).wait_send()
@@ -647,10 +627,13 @@
     shape = jax.ShapeDtypeStruct
     vmem = pl.BlockSpec(memory_space=pltpu.VMEM)
     smem = pl.BlockSpec(memory_space=pltpu.SMEM)
-    flat = lambda x: x.reshape(-1, LANES)
+    flat = lambda x: stay(x.reshape(-1, LANES))
     slots = (SLOT_ROWS, LANES)
     messages = pltpu.VMEM((PEERS * MSG_ROWS, LANES), F32)
-    anywhere = pl.BlockSpec(memory_space=pl.ANY)
+    hbm = pl.BlockSpec(memory_space=pltpu.HBM)
+    entries = pltpu.VMEM((96, LANES), I32)
+    stay = lambda x: pltpu.with_memory_space_constraint(x, pltpu.HBM)
+    far = lambda x: stay(tiles_of(x))
     columns, cells = pltpu.VMEM((1024, LANES), F32), pltpu.VMEM((768, LANES), F32)
     lowest, soil, factor, reduced = call(
         step_kernel,
@@ -659,14 +642,18 @@
             shape((2, 1024, LANES), F32), shape((4, 1024, LANES), F32),
         ],
         [
+            entries, entries, entries, entries,
+            pltpu.VMEM((2, LANES), F32),
+            pltpu.VMEM((3, 96 * LANES), F32),
+            pltpu.VMEM((96, LANES), F32),
+            entries,
             pltpu.VMEM((4, 1024, LANES), F32),
             columns, columns, columns, cells, cells, cells,
-            pltpu.SemaphoreType.DMA((9,)),
+            pltpu.SemaphoreType.DMA((15,)),
+            pltpu.VMEM((3, 96, LANES), F32),
             pltpu.VMEM(slots, I32),
             pltpu.VMEM(slots, F32),
             pltpu.VMEM(slots, F32),
-            pltpu.VMEM((2, 1024, LANES), F32),
-            pltpu.VMEM((4, 1024, LANES), F32),
             pltpu.VMEM((6, 16, LANES), F32),
             pltpu.VMEM((5, 96, LANES), F32),
             pltpu.VMEM((96, LANES), F32),
@@ -684,30 +671,25 @@
             pltpu.SemaphoreType.DMA((CHUNKS,)),
             pltpu.SemaphoreType.DMA((CHUNKS,)),
         ],
-        [vmem] * 5 + [anywhere] * 4 + [smem] + [anywhere] * 3 + [vmem] * 3,
-        [vmem] * 2 + [anywhere] * 2,
+        [hbm] * 9 + [smem] + [hbm] * 6,
+        [vmem] * 4,
         collective_id=0, has_side_effects=True,
     )(
         flat(entry_owner), flat(entry_cell), flat(entry_column), flat(entry_area), flat(area_table),
-        tiles_of(profiles), tiles_of(heat_coupling), tiles_of(momentum_coupling), tiles_of(layer_mass),
-        layer_counts, tiles_of(soil_temps), tiles_of(heat_capacity), tiles_of(conductance),
-        exchange_coeffs.reshape(3, 96, LANES), flat(wetness), flat(surface_type),
+        far(profiles), far(heat_coupling), far(momentum_coupling), far(layer_mass),
+        stay(layer_counts), far(soil_temps), far(heat_capacity), far(conductance),
+        stay(exchange_coeffs), flat(wetness), flat(surface_type),
     )
     new_profiles, new_soil = call(
         up_kernel,
         [shape((4, 1024, LANES), F32), shape((768, LANES), F32)],
         [
-            pltpu.VMEM((2, 1024, LANES), F32),
             pltpu.VMEM((4, 1024, LANES), F32),
-            pltpu.VMEM((4, 1024, LANES), F32),
-            cells,
-            pltpu.SemaphoreType.DMA((2,)),
-            pltpu.SemaphoreType.DMA((8,)),
-            pltpu.SemaphoreType.DMA((8,)),
+            pltpu.SemaphoreType.DMA,
             pltpu.SemaphoreType.DMA((8,)),
         ],
-        [vmem] + [anywhere] * 3,
-        [anywhere] * 2,
+        [vmem] * 4,
+        [hbm] * 2,
     )(lowest, factor, reduced, soil)
     return untile(new_profiles, 64, 2048), untile(new_soil, 8, 12288)
 

time: 50.6 us -> 46.3 us (0.915)
  Pallas kernels: 47.9 us -> 45.4 us
  local copies, waits for them, and re-layouts: 1.6 us -> 0 us
    pallas_call x1, Pallas kernels: 4.11 us -> 1.59 us  [local(): call(up_kernel, [shape((4, 1024, LANES), F32), shape((768, LANES), F32)],...]
    unnamed x1 -> x0, local copies, waits for them, and re-layouts: 1.6 us -> none
where the time goes in v4:
time: 46.3 us; the launch traced here: 46.2 us
  Pallas kernels  45.4 us (98%)
  between operations  0.81 us (2%)
    pallas_call x1, Pallas kernels, local(): call(step_kernel, [shape((4, 16, LANES), F32), shape((768, LANES), F32),...  43.8 us
    pallas_call x1, Pallas kernels, local(): call(up_kernel, [shape((4, 1024, LANES), F32), shape((768, LANES), F32)],...  1.59 us

profile of v4, /device:TPU:1, one launch (start us, length us, event | category | flops | bytes accessed | tf_op | source)
XLA Modules:
  0.0 46.2 jit_solution(16440963784717293626)
XLA Ops:
  0.6 43.8 %shard_map.167 = (f32[4,16,128]{2,1,0:T(8,128)S(1)}, f32[768,128]{1,0:T(8,128)S(1)}, f32[2,1024,128]{2,1,0:T(8,128)S(1)}, f32[4,1024,128]{2,1,0:T(8,128)S(1)}) custom-call(s32[96,128]{1,0:T(8,128)} %bitcast.59, s32[96,128]{1,0:T(8,128)} %bitcast.60, s32[96,128]{1,0:T(8,128)} %bitcast.61, s32[96,128]{1,0:T(8,128)} %bitcast.62, f32[2,128]{1,0:T(2,128)} %bitcast.65, ...), custom_call_target="tpu_custom_call" | custom-call | tf_op jit(solution)/shard_map/pallas_call | solution.py:638
  44.4 1.6 %shard_map.168 = (f32[4,1024,128]{2,1,0:T(8,128)}, f32[768,128]{1,0:T(8,128)}) custom-call(f32[4,16,128]{2,1,0:T(8,128)S(1)} %get-tuple-element.8.lowest_ref, f32[2,1024,128]{2,1,0:T(8,128)S(1)} %get-tuple-element.9.factor_ref, f32[4,1024,128]{2,1,0:T(8,128)S(1)} %get-tuple-element.10.reduced_ref, f32[768,128]{1,0:T(8,128)S(1)} %get-tuple-element.11.soil_ref), custom_call_target="tpu_custom_call" | custom-call | tf_op jit(solution)/shard_map/pallas_call | solution.py:683

commit v5 on v4

--- a/solution.py
+++ b/solution.py
@@ -13,7 +13,7 @@
 REPLY_ROWS = 5
 CHUNKS = 4
 CHUNK_PEERS = PEERS // CHUNKS
-LAG = 3
+LAG = 4
 PIECES = 2
 BF16 = jnp.bfloat16
 F32 = jnp.float32
@@ -116,7 +116,7 @@
             onehot = onehot_rows(owner_ref[pl.ds(r, 1), :], PEERS)
             lefts.append(jnp.concatenate([
                 onehot * jnp.broadcast_to(piece_scr[p, pl.ds(r, 1), :], (PEERS, LANES)).astype(BF16)
-                for p in range(5)
+                for p in range(3)
             ], axis=0))
             rights.append((ranks == rank_scr[pl.ds(r, 1), :]).astype(F32).astype(BF16))
         acc_scr[...] += dot_nt(jnp.concatenate(lefts, axis=1), jnp.concatenate(rights, axis=1))
@@ -173,18 +173,36 @@
         bottom_scr[5, rows, :] = inverse[2 + half]
 
 
+def encode(number, bits):
+    value = ((number & 127) + 128).astype(F32) * (2.0**-64 if bits == 7 else 1.0)
+    for b in range(bits):
+        value = value * jnp.where(((number >> (7 + b)) & 1) == 1, 2.0 ** (2**b), 1.0)
+    return value
+
+
+def decode(value, bits):
+    filled = value > 0.0
+    row = jnp.zeros(value.shape, I32)
+    if bits == 7:
+        large = value >= 128.0
+        row = jnp.where(large, 64, 0)
+        value = jnp.where(large, value, value * 2.0**64)
+        bits = 6
+    for b in range(bits - 1, -1, -1):
+        large = value >= 128.0 * 2.0 ** (2**b)
+        row = jnp.where(large, row + 2**b, row)
+        value = jnp.where(large, value * 2.0 ** -(2**b), value)
+    return row, jnp.where(filled, value - 128.0, 0.0).astype(I32), filled
+
+
 def prepare_pieces(cell_ref, column_ref, area_ref, piece_scr):
-    cell = cell_ref[...]
-    column = column_ref[...]
-    piece_scr[0] = ((cell >> 8) + 1).astype(F32)
-    piece_scr[1] = (cell & 255).astype(F32)
-    piece_scr[2] = (column >> 7).astype(F32)
-    piece_scr[3] = (column & 127).astype(F32)
-    piece_scr[4] = area_ref[...].astype(F32)
+    piece_scr[0] = encode(cell_ref[...], 7)
+    piece_scr[1] = encode(column_ref[...], 4)
+    piece_scr[2] = area_ref[...].astype(F32)
 
 
 def prepare_group(
-    j, acc_scr, table_ref, bottom_ref, field_scr, column_slot_ref, weight_slot_ref, wind_slot_ref, send_scr
+    j, acc_scr, table_ref, bottom_ref, field_scr, column_slot_ref, weight_slot_ref, send_scr
 ):
     near_table = jnp.broadcast_to(table_ref[0:1, :], (8, LANES))
     far_table = jnp.broadcast_to(table_ref[1:2, :], (8, LANES))
@@ -198,30 +216,47 @@
         return acc_scr[near, 0:LANES], acc_scr[far, 0:LANES], last
 
     highs, lows = [], []
-    for k, (cell_high, cell_low, row, lane, area) in enumerate(zip(*[pieces(p) for p in range(5)])):
+    for k, (cell, column, area) in enumerate(zip(*[pieces(p) for p in range(3)])):
         rows = pl.ds(base + 8 * k, 8)
-        field_scr[0, rows, :] = cell_high * 256.0 + cell_low
-        row, lane, area = row.astype(I32), lane.astype(I32), area.astype(I32)
-        column_slot_ref[rows, :] = row * LANES + lane
+        row, lane, filled = decode(cell, 7)
+        field_scr[0, rows, :] = jnp.where(filled, row * LANES + lane + 256, 0).astype(F32)
+        area = area.astype(I32)
         weight = jnp.where(
             area < LANES, lane_gather(near_table, area & 127), lane_gather(far_table, area & 127)
         )
-        weight_slot_ref[rows, :] = jnp.where(cell_high > 0.0, weight, 0.0)
+        weight_slot_ref[rows, :] = jnp.where(filled, weight, 0.0)
+        row, lane, _ = decode(column, 4)
+        column_slot_ref[rows, :] = row * LANES + lane
         highs.append(row)
         lows.append(lane)
-    totals = [[jnp.zeros((8, LANES), F32) for _ in range(4)] for _ in range(3)]
+    totals = expand(bottom_ref, (0, 1, 4), highs, lows)
+    for k in range(3):
+        for f in range(3):
+            field_scr[f + 1, pl.ds(base + 8 * k, 8), :] = totals[k][f]
+    pack_group(j, [field_scr.at[f] for f in range(4)], base, send_scr)
+
+
+def expand(bottom_ref, fields, highs, lows):
+    totals = [[jnp.zeros((8, LANES), F32) for _ in fields] for _ in highs]
     for h in range(16):
-        tables = [jnp.broadcast_to(bottom_ref[f, h : h + 1, :], (8, LANES)) for f in (0, 1, 4, 5)]
-        for k in range(3):
+        tables = [jnp.broadcast_to(bottom_ref[f, h : h + 1, :], (8, LANES)) for f in fields]
+        for k in range(len(highs)):
             hit = highs[k] == h
-            for f in range(4):
-                totals[k][f] = jnp.where(hit, lane_gather(tables[f], lows[k]), totals[k][f])
-    for k in range(3):
-        rows = pl.ds(base + 8 * k, 8)
-        for f in range(3):
-            field_scr[f + 1, rows, :] = totals[k][f]
-        wind_slot_ref[rows, :] = totals[k][3]
-    pack_group(j, [field_scr.at[f] for f in range(4)], base, send_scr)
+            for f, table in enumerate(tables):
+                totals[k][f] = jnp.where(hit, lane_gather(table, lows[k]), totals[k][f])
+    return totals
+
+
+def expand_wind(bottom_ref, column_slot_ref, wind_slot_ref):
+    def body(step, carry):
+        blocks = [pl.ds(aligned(step, 48) + 8 * k, 8) for k in range(6)]
+        columns = [column_slot_ref[rows, :] for rows in blocks]
+        totals = expand(bottom_ref, (5,), [x >> 7 for x in columns], [x & 127 for x in columns])
+        for rows, (value,) in zip(blocks, totals):
+            wind_slot_ref[rows, :] = value
+        return carry
+
+    lax.fori_loop(0, 4, body, 0)
 
 
 def soil_block(a, b, soil_ref, capacity_ref, conductance_ref, exchange_ref, wetness_ref, type_ref, counts_ref,
@@ -513,7 +548,7 @@
         for j in groups_of(ahead(i)):
             prepare_group(
                 j, slot_acc_scr, table_ref, bottom_scr, field_scr, column_slot_scr, weight_slot_scr,
-                wind_slot_scr, send_scr,
+                send_scr,
             )
 
     def send(i, own):
@@ -573,6 +608,7 @@
         return carry
 
     lax.fori_loop(1, LAG, ask, 0)
+    expand_wind(bottom_scr, column_slot_scr, wind_slot_scr)
 
     def back(i, carry):
         gather(i, False)
@@ -655,9 +691,9 @@
             pltpu.VMEM(slots, F32),
             pltpu.VMEM(slots, F32),
             pltpu.VMEM((6, 16, LANES), F32),
-            pltpu.VMEM((5, 96, LANES), F32),
+            pltpu.VMEM((3, 96, LANES), F32),
             pltpu.VMEM((96, LANES), F32),
-            pltpu.VMEM((5 * PEERS, 256), F32),
+            pltpu.VMEM((3 * PEERS, 256), F32),
             pltpu.VMEM((4,) + slots, F32),
             pltpu.VMEM((4 * PIECES,) + slots, F32),
             pltpu.VMEM((144 * PIECES, 256), F32),

time: 46.3 us -> 43.9 us (0.948)
  Pallas kernels: 45.4 us -> 43.2 us
    pallas_call x1, Pallas kernels: 43.8 us -> 41.6 us  [local(): call(step_kernel, [shape((4, 16, LANES), F32), shape((768, LANES), F32),...]
where the time goes in v5:
time: 43.9 us; the launch traced here: 43.8 us
  Pallas kernels  43.2 us (98%)
  between operations  0.65 us (1%)
    pallas_call x1, Pallas kernels, local(): call(step_kernel, [shape((4, 16, LANES), F32), shape((768, LANES), F32),...  41.6 us
    pallas_call x1, Pallas kernels, local(): call(up_kernel, [shape((4, 1024, LANES), F32), shape((768, LANES), F32)],...  1.59 us

profile of v5, /device:TPU:1, one launch (start us, length us, event | category | flops | bytes accessed | tf_op | source)
XLA Modules:
  0.0 43.8 jit_solution(8467399442143140995)
XLA Ops:
  0.6 41.6 %shard_map.167 = (f32[4,16,128]{2,1,0:T(8,128)S(1)}, f32[768,128]{1,0:T(8,128)S(1)}, f32[2,1024,128]{2,1,0:T(8,128)S(1)}, f32[4,1024,128]{2,1,0:T(8,128)S(1)}) custom-call(s32[96,128]{1,0:T(8,128)} %bitcast.59, s32[96,128]{1,0:T(8,128)} %bitcast.60, s32[96,128]{1,0:T(8,128)} %bitcast.61, s32[96,128]{1,0:T(8,128)} %bitcast.62, f32[2,128]{1,0:T(2,128)} %bitcast.65, ...), custom_call_target="tpu_custom_call" | custom-call | tf_op jit(solution)/shard_map/pallas_call | solution.py:674
  42.2 1.6 %shard_map.168 = (f32[4,1024,128]{2,1,0:T(8,128)}, f32[768,128]{1,0:T(8,128)}) custom-call(f32[4,16,128]{2,1,0:T(8,128)S(1)} %get-tuple-element.8.lowest_ref, f32[2,1024,128]{2,1,0:T(8,128)S(1)} %get-tuple-element.9.factor_ref, f32[4,1024,128]{2,1,0:T(8,128)S(1)} %get-tuple-element.10.reduced_ref, f32[768,128]{1,0:T(8,128)S(1)} %get-tuple-element.11.soil_ref), custom_call_target="tpu_custom_call" | custom-call | tf_op jit(solution)/shard_map/pallas_call | solution.py:719

commit v6 on v5

--- a/solution.py
+++ b/solution.py
@@ -83,13 +83,12 @@
     return (iota((count, LANES), 0) == ids).astype(F32).astype(BF16)
 
 
-def rank_entries(owner_ref, rank_scr, greet):
+def rank_entries(owner_ref, rank_scr):
     upper = (iota((LANES, 2 * LANES), 0) < iota((LANES, 2 * LANES), 1)).astype(F32).astype(BF16)
     owners = iota((PEERS, LANES), 0)
     block = 32
 
     def body(step, base):
-        greet(step)
         hits = [owners == owner_ref[pl.ds(step * block + q, 1), :] for q in range(block)]
         onehots = jnp.concatenate([hit.astype(F32).astype(BF16) for hit in hits], axis=0)
         before = jnp.dot(onehots, upper, preferred_element_type=F32)
@@ -461,12 +460,17 @@
     return (peer // 32, lax.rem(peer, 32))
 
 
-def greet(me, first, count):
-    barrier = pltpu.get_barrier_semaphore()
-    for k in range(count):
+def mates():
+    group, tile = lax.axis_index("grp"), lax.axis_index("tile")
+    row = [(group, lax.rem(tile + k, 32)) for k in range(1, 32)]
+    column = [(lax.rem(group + k, 4), tile) for k in range(1, 4)]
+    return row, column
+
+
+def signal(semaphore, devices):
+    for device in devices:
         pl.semaphore_signal(
-            barrier, inc=1, device_id=device_of(lax.rem(me + first + k, PEERS)),
-            device_id_type=pl.DeviceIdType.MESH,
+            semaphore, inc=1, device_id=device, device_id_type=pl.DeviceIdType.MESH
         )
 
 
@@ -504,7 +508,7 @@
     column_slot_scr, weight_slot_scr, wind_slot_scr, bottom_scr,
     piece_scr, rank_scr, slot_acc_scr, field_scr, slot_piece_scr, cell_acc_scr, cells_scr, table_scr,
     table_piece_scr, index_scr, column_acc_scr, send_scr, recv_scr, reply_scr, return_scr,
-    sent_sem, there_sems, back_sems,
+    sent_sem, there_sems, back_sems, rows_sem,
 ):
     me = lax.axis_index("grp") * 32 + lax.axis_index("tile")
     mine = lax.rem(me, 64) // (CHUNK_PEERS // 2)
@@ -521,12 +525,16 @@
     entry_loads, column_loads, soil_loads = loads[:4], loads[4:10], loads[10:]
     for load in loads:
         load.start()
-    greet(me, 1, 1)
+    barrier = pltpu.get_barrier_semaphore()
+    row_mates, column_mates = mates()
+    signal(barrier, column_mates + row_mates)
     for load in entry_loads:
         load.wait()
     prepare_pieces(cell_ref, column_ref, area_ref, piece_scr)
-    rank_entries(owner_ref, rank_scr, lambda step: greet(me, 2 + 42 * step, 42))
+    rank_entries(owner_ref, rank_scr)
     assign_slots(owner_ref, rank_scr, piece_scr, slot_acc_scr)
+    pl.semaphore_wait(barrier, 34)
+    signal(rows_sem, column_mates)
     for load in column_loads:
         load.wait()
     for row in range(3):
@@ -562,7 +570,7 @@
         scatter_group(groups_of(chunk), recv_scr, index_scr, slot_piece_scr, cell_acc_scr)
 
     prepare(0)
-    pl.semaphore_wait(pltpu.get_barrier_semaphore(), PEERS - 1)
+    pl.semaphore_wait(rows_sem, 3)
     send(0, True)
 
     def there(i, carry):
@@ -706,6 +714,7 @@
             pltpu.SemaphoreType.DMA((2,)),
             pltpu.SemaphoreType.DMA((CHUNKS,)),
             pltpu.SemaphoreType.DMA((CHUNKS,)),
+            pltpu.SemaphoreType.REGULAR,
         ],
         [hbm] * 9 + [smem] + [hbm] * 6,
         [vmem] * 4,

time: 43.9 us -> 42.6 us (0.970)
  Pallas kernels: 43.2 us -> 41.8 us
    pallas_call x1, Pallas kernels: 41.6 us -> 40.2 us  [local(): call(step_kernel, [shape((4, 16, LANES), F32), shape((768, LANES), F32),...]
where the time goes in v6:
time: 42.6 us; the launch traced here: 42.5 us
  Pallas kernels  41.8 us (98%)
  between operations  0.65 us (2%)
    pallas_call x1, Pallas kernels, local(): call(step_kernel, [shape((4, 16, LANES), F32), shape((768, LANES), F32),...  40.2 us
    pallas_call x1, Pallas kernels, local(): call(up_kernel, [shape((4, 1024, LANES), F32), shape((768, LANES), F32)],...  1.59 us

profile of v6, /device:TPU:1, one launch (start us, length us, event | category | flops | bytes accessed | tf_op | source)
XLA Modules:
  0.0 42.5 jit_solution(3954398317035520621)
XLA Ops:
  0.6 40.2 %shard_map.167 = (f32[4,16,128]{2,1,0:T(8,128)S(1)}, f32[768,128]{1,0:T(8,128)S(1)}, f32[2,1024,128]{2,1,0:T(8,128)S(1)}, f32[4,1024,128]{2,1,0:T(8,128)S(1)}) custom-call(s32[96,128]{1,0:T(8,128)} %bitcast.59, s32[96,128]{1,0:T(8,128)} %bitcast.60, s32[96,128]{1,0:T(8,128)} %bitcast.61, s32[96,128]{1,0:T(8,128)} %bitcast.62, f32[2,128]{1,0:T(2,128)} %bitcast.65, ...), custom_call_target="tpu_custom_call" | custom-call | tf_op jit(solution)/shard_map/pallas_call | solution.py:682
  40.9 1.6 %shard_map.168 = (f32[4,1024,128]{2,1,0:T(8,128)}, f32[768,128]{1,0:T(8,128)}) custom-call(f32[4,16,128]{2,1,0:T(8,128)S(1)} %get-tuple-element.8.lowest_ref, f32[2,1024,128]{2,1,0:T(8,128)S(1)} %get-tuple-element.9.factor_ref, f32[4,1024,128]{2,1,0:T(8,128)S(1)} %get-tuple-element.10.reduced_ref, f32[768,128]{1,0:T(8,128)S(1)} %get-tuple-element.11.soil_ref), custom_call_target="tpu_custom_call" | custom-call | tf_op jit(solution)/shard_map/pallas_call | solution.py:728
